TPU v7x, 32 devices: a whole 2x2x4 slice. The times are simulated.
32 devices in a mesh: shard: 2 (over x), ctx: 4 (over y, core), tp: 4 (over z).
Axes of the slice: x: 2, y: 2, z: 4, core: 2. Of those that a mesh axis runs over, the one named last changes fastest.
Arguments:
- tokens: bfloat16 [8, 1024, 767], P('shard', 'ctx'), may hold values from -6 to 6
- lengths: int32 [8], P('shard'), may hold values from 256 to 1024, as said below
- first_gain: float32 [768], replicated, may hold values from 0.5 to 1.5
- entry_weight: bfloat16 [3, 768, 768], P(None, ('shard', 'ctx'), 'tp'), may hold values from -0.21875 to 0.21875
- entry_bias: float32 [2, 768], P(None, 'tp'), may hold values from -3 to 3
- exit_weight: bfloat16 [768, 768], P('tp', ('shard', 'ctx')), may hold values from -0.625 to 0.625
- exit_bias: float32 [768], replicated, may hold values from -3 to 3
- second_gain: float32 [768], replicated, may hold values from 0.5 to 1.5
- hidden_weight: bfloat16 [768, 3072], P(('shard', 'ctx'), 'tp'), may hold values from -0.21875 to 0.21875
- hidden_bias: float32 [3072], P('tp'), may hold values from -3 to 3
- return_weight: bfloat16 [3072, 768], P('tp', ('shard', 'ctx')), may hold values from -0.109375 to 0.109375
- return_bias: float32 [768], replicated, may hold values from -3 to 3
- cotangent: bfloat16 [8, 1024, 767], P('shard', 'ctx'), may hold values from -6 to 6
Outputs:
- result: bfloat16 [8, 1024, 767], P('shard', 'ctx')
- tokens_gradient: bfloat16 [8, 1024, 767], P('shard', 'ctx')
- first_gain_gradient: float32 [768], replicated
- entry_weight_gradient: float32 [3, 768, 768], P(None, ('shard', 'ctx'), 'tp')
- entry_bias_gradient: float32 [2, 768], P(None, 'tp')
- exit_weight_gradient: float32 [768, 768], P('tp', ('shard', 'ctx'))
- exit_bias_gradient: float32 [768], replicated
- second_gain_gradient: float32 [768], replicated
- hidden_weight_gradient: float32 [768, 3072], P(('shard', 'ctx'), 'tp')
- hidden_bias_gradient: float32 [3072], P('tp')
- return_weight_gradient: float32 [3072, 768], P('tp', ('shard', 'ctx'))
- return_bias_gradient: float32 [768], replicated
Inputs may be any that keep to these rules, and one draw needn't show every extreme that they name: `lengths`: in every draw some sequence has exactly 1024 valid positions and some has exactly 256.
All inputs are finite; a program needn't handle non-finite values.
Results may differ from a plain program's by a relative error of at most 0.014.
Values may be sent and summed in bfloat16 or wider, within the bound.
No kernel may reach another device: no remote copies, remote signals or barrier semaphores. Data moves between devices by JAX's collectives and lax.ppermute only.
A program may use at most 256 MiB of HBM per device.

v0:
```python
import functools
import math

import jax
import jax.numpy as jnp
from jax import lax
from jax.experimental import pallas as pl
from jax.experimental.pallas import tpu as pltpu
from jax.sharding import PartitionSpec as P

HDIM = 64
PAIR = 2 * HDIM
EPSILON = 1e-05
MASKED = -1e30
LOW = jnp.bfloat16
SINGLE = jnp.float32


def row_mean(values):
    return jnp.mean(values, -1, keepdims=True)


def dot(left, right):
    return jnp.dot(left, right, preferred_element_type=SINGLE)


def dot_nt(left, right):
    return lax.dot_general(left, right, (((1,), (1,)), ((), ())), preferred_element_type=SINGLE)


def dot_tn(left, right):
    return lax.dot_general(left, right, (((0,), (0,)), ((), ())), preferred_element_type=SINGLE)


def key_positions(meta, block, local, upper):
    base = upper * 2 * local + (meta[1] ^ block) * local
    return base + lax.broadcasted_iota(jnp.int32, (local, 1), 0)


def query_positions(meta, block, local):
    base = meta[0] * 2 * local + (meta[1] ^ block) * local
    return base + lax.broadcasted_iota(jnp.int32, (1, local), 1)


def near_mask(meta, block, local):
    position = jnp.concatenate([key_positions(meta, b, local, meta[0]) for b in (0, 1)], 0)
    return (position <= query_positions(meta, block, local)) & (position < meta[2])


def far_mask(meta, local):
    position = jnp.concatenate([key_positions(meta, b, local, 0) for b in (0, 1)], 0)
    return position < jnp.where(meta[0] == 1, meta[2], 0)


def half_of(values, head):
    lanes = lax.broadcasted_iota(jnp.int32, values.shape, 1)
    return jnp.where(lanes // HDIM == head, values, jnp.zeros_like(values))


def each_head(local, body):
    @pl.loop(0, 4)
    def _(at):
        block, head = at // 2, at % 2
        body(block, head, pl.ds(pl.multiple_of(block * local, local), local), pl.ds(head, 1))


def prepare_kernel(
    meta, tokens_ref, cot_ref, gain_ref, stream_ref, unit_ref, inverse_ref, cot_out_ref, normed_ref,
    two_ref
):
    local, narrow = tokens_ref.shape
    inside = lax.broadcasted_iota(jnp.int32, (local, narrow + 1), 1) < narrow
    stream_ref[:, :narrow] = tokens_ref[...].astype(SINGLE)
    part = jnp.where(inside, stream_ref[...], 0.0)
    stream = jnp.where(inside, part, -jnp.sum(part, -1, keepdims=True))
    inverse = lax.rsqrt(row_mean(stream * stream) + EPSILON)
    unit = stream * inverse
    normed = (unit * gain_ref[...]).astype(LOW)
    stream_ref[...] = stream
    unit_ref[...] = unit
    inverse_ref[...] = inverse
    normed_ref[...] = normed
    two_ref[:, : narrow + 1] = normed
    position = meta[3] * local + lax.broadcasted_iota(jnp.int32, (local, 1), 0)
    cot_out_ref[:, :narrow] = cot_ref[...].astype(SINGLE)
    cot = jnp.where(inside & (position < meta[2]), cot_out_ref[...], 0.0)
    cot_out_ref[...] = cot
    two_ref[:, narrow + 1 :] = (cot - row_mean(cot)).astype(LOW)


def prepare(meta, tokens, cotangent, gain):
    local, narrow = tokens.shape
    wide = narrow + 1
    outs = [(wide, SINGLE), (wide, SINGLE), (1, SINGLE), (wide, SINGLE), (wide, LOW), (2 * wide, LOW)]
    own = pl.BlockSpec((local, narrow), lambda j, meta: (0, 0))
    return pl.pallas_call(
        prepare_kernel,
        grid_spec=pltpu.PrefetchScalarGridSpec(
            num_scalar_prefetch=1,
            grid=(1,),
            in_specs=[own, own, pl.BlockSpec((1, wide), lambda j, meta: (0, 0))],
            out_specs=[pl.BlockSpec((local, size), lambda j, meta: (0, 0)) for size, _ in outs],
        ),
        out_shape=[jax.ShapeDtypeStruct((local, size), dtype) for size, dtype in outs],
        cost_estimate=pl.CostEstimate(
            flops=20 * local * wide, bytes_accessed=20 * local * wide, transcendentals=local
        ),
        name="prepare",
    )(meta, tokens, cotangent, gain)


def forward_kernel(meta, q_ref, k_ref, v_ref, kf_ref, vf_ref, out_ref, log_ref, mix):
    local = q_ref.shape[0] // 2
    scale = jnp.asarray(1.0 / math.sqrt(HDIM), LOW)
    mix[...] = jnp.zeros_like(mix)

    def body(block, head, rows, line):
        near, far = near_mask(meta, block, local), far_mask(meta, local)
        query = half_of(q_ref[rows, :], head) * scale
        near_s = jnp.where(near, dot_nt(k_ref[...], query), MASKED)
        far_s = jnp.where(far, dot_nt(kf_ref[...], query), MASKED)
        top = jnp.maximum(jnp.max(near_s, 0, keepdims=True), jnp.max(far_s, 0, keepdims=True))
        near_p = jnp.exp(near_s - top)
        far_p = jnp.exp(far_s - top)
        total = jnp.sum(near_p, 0, keepdims=True) + jnp.sum(far_p, 0, keepdims=True)
        mixed = dot_tn(half_of(v_ref[...], head), near_p.astype(LOW))
        mixed = mixed + dot_tn(half_of(vf_ref[...], head), far_p.astype(LOW))
        mix[:, rows] += mixed / total
        log_ref[0, line, rows] = top + jnp.log(total)

    each_head(local, body)
    out_ref[...] = mix[...].T.astype(LOW)


def far_backward_kernel(
    meta, q_ref, k_ref, v_ref, grad_ref, out_ref, log_ref, dkv_ref, inner_ref, mix_ref, sums
):
    width = dkv_ref.shape[1] // 2
    local = q_ref.shape[0] // 2
    scale = jnp.asarray(1.0 / math.sqrt(HDIM), LOW)
    sums[...] = jnp.zeros_like(sums)
    mix_ref[...] = jnp.zeros_like(mix_ref)

    def body(block, head, rows, line):
        mask = far_mask(meta, local)
        query = half_of(q_ref[rows, :], head) * scale
        out_grad = half_of(grad_ref[rows, :], head)
        inner = out_grad.astype(SINGLE) * out_ref[rows, :].astype(SINGLE)
        inner = jnp.sum(inner.T, 0, keepdims=True)
        inner_ref[0, line, rows] = inner
        scores = jnp.where(mask, dot_nt(k_ref[...], query), MASKED)
        probs = jnp.exp(scores - log_ref[0, line, rows])
        grads = (probs * (dot_nt(v_ref[...], out_grad) - inner)).astype(LOW)
        sums[0] += dot(grads, query)
        sums[1] += dot(probs.astype(LOW), out_grad)
        mix_ref[0, :, rows] += dot_tn(half_of(k_ref[...], head), grads)

    each_head(local, body)
    lanes = pl.multiple_of(pl.program_id(0) * PAIR, PAIR)
    dkv_ref[:, pl.ds(lanes, PAIR)] = sums[0].astype(LOW)
    dkv_ref[:, pl.ds(width + lanes, PAIR)] = sums[1].astype(LOW)


def near_backward_kernel(
    meta, q_ref, k_ref, v_ref, grad_ref, log_ref, inner_ref, mix_ref, out_ref, sums, mix
):
    width = out_ref.shape[1] // 3
    local = q_ref.shape[0] // 2
    scale = 1.0 / math.sqrt(HDIM)
    sums[...] = jnp.zeros_like(sums)
    mix[...] = mix_ref[0]

    def body(block, head, rows, line):
        mask = near_mask(meta, block, local)
        query = half_of(q_ref[rows, :], head) * jnp.asarray(scale, LOW)
        out_grad = half_of(grad_ref[rows, :], head)
        scores = jnp.where(mask, dot_nt(k_ref[...], query), MASKED)
        probs = jnp.exp(scores - log_ref[0, line, rows])
        inner = inner_ref[0, line, rows]
        grads = (probs * (dot_nt(v_ref[...], out_grad) - inner)).astype(LOW)
        sums[0] += dot(grads, query)
        sums[1] += dot(probs.astype(LOW), out_grad)
        mix[:, rows] += dot_tn(half_of(k_ref[...], head), grads)

    each_head(local, body)
    lanes = pl.multiple_of(pl.program_id(0) * PAIR, PAIR)
    out_ref[:, pl.ds(lanes, PAIR)] = (mix[...] * scale).T.astype(LOW)
    out_ref[:, pl.ds(width + lanes, PAIR)] = sums[0].astype(LOW)
    out_ref[:, pl.ds(2 * width + lanes, PAIR)] = sums[1].astype(LOW)


def attention_call(kernel, name, meta, rows, width, operands, outs, scratch=()):
    pairs = width // PAIR
    part = lambda at: ((rows, PAIR), lambda j, meta: (0, at * pairs + j), (rows, width))
    specs = {
        0: part(0),
        1: part(1),
        2: part(2),
        "row": ((1, 2, rows), lambda j, meta: (j, 0, 0), (pairs, 2, rows)),
        "mix": ((1, PAIR, rows), lambda j, meta: (j, 0, 0), (pairs, PAIR, rows)),
        "two": ((rows, 2 * width), lambda j, meta: (0, 0), (rows, 2 * width)),
        "three": ((rows, 3 * width), lambda j, meta: (0, 0), (rows, 3 * width)),
    }
    return pl.pallas_call(
        kernel,
        grid_spec=pltpu.PrefetchScalarGridSpec(
            num_scalar_prefetch=1,
            grid=(pairs,),
            in_specs=[pl.BlockSpec(*specs[kind][:2]) for kind, _ in operands],
            out_specs=[pl.BlockSpec(*specs[kind][:2]) for kind, _ in outs],
            scratch_shapes=list(scratch),
        ),
        out_shape=[jax.ShapeDtypeStruct(specs[kind][2], dtype) for kind, dtype in outs],
        cost_estimate=pl.CostEstimate(
            flops=8 * rows * rows * width, bytes_accessed=rows * width * 16,
            transcendentals=rows * rows * width // HDIM,
        ),
        name=name,
    )(meta, *(array for _, array in operands))


def attend(meta, width, near, far_kv):
    return attention_call(
        forward_kernel, "attend", meta, near.shape[0], width,
        [(0, near), (1, near), (2, near), (0, far_kv), (1, far_kv)],
        [(0, LOW), ("row", SINGLE)],
        [pltpu.VMEM((PAIR, near.shape[0]), SINGLE)],
    )


def attend_far_back(meta, width, near, far_kv, grads, attended, logs):
    rows = near.shape[0]
    return attention_call(
        far_backward_kernel, "attend_far_back", meta, rows, width,
        [(0, near), (0, far_kv), (1, far_kv), (0, grads), (0, attended), ("row", logs)],
        [("two", LOW), ("row", SINGLE), ("mix", SINGLE)],
        [pltpu.VMEM((2, rows, PAIR), SINGLE)],
    )


def attend_near_back(meta, width, near, grads, logs, inner, mixed):
    rows = near.shape[0]
    return attention_call(
        near_backward_kernel, "attend_near_back", meta, rows, width,
        [(0, near), (1, near), (2, near), (0, grads), ("row", logs), ("row", inner),
         ("mix", mixed)],
        [("three", LOW)],
        [pltpu.VMEM((2, rows, PAIR), SINGLE), pltpu.VMEM((PAIR, rows), SINGLE)],
    )[0]


def after(value, *gates):
    return lax.optimization_barrier((value, *gates))[0]


class Place:
    def __init__(self):
        self.n_shard = lax.axis_size("shard")
        self.n_ctx = lax.axis_size("ctx")
        self.n_tp = lax.axis_size("tp")
        self.shard = lax.axis_index("shard")
        self.ctx = lax.axis_index("ctx")
        self.half = self.ctx // 2
        self.core = self.ctx % 2
        self.tp = lax.axis_index("tp")
        self.home = self.core == self.tp // 2

    def core_swap(self, value):
        return lax.ppermute(value, "ctx", [(i, i ^ 1) for i in range(self.n_ctx)])

    def half_swap(self, value):
        return lax.ppermute(value, "ctx", [(i, i ^ 2) for i in range(self.n_ctx)])

    def half_up(self, value):
        return lax.ppermute(value, "ctx", [(0, 2), (1, 3)])

    def half_down(self, value):
        return lax.ppermute(value, "ctx", [(2, 0), (3, 1)])

    def shard_swap(self, value):
        return lax.ppermute(value, "shard", [(0, 1), (1, 0)])

    def tp_swap(self, value, mask):
        return lax.ppermute(value, "tp", [(i, i ^ mask) for i in range(self.n_tp)])

    def ordered(self, flag, mine, other, axis=0):
        first = jnp.where(flag == 0, mine, other)
        second = jnp.where(flag == 0, other, mine)
        return jnp.stack([first, second], axis)


    def own_block(self, piece, far):
        kept = jnp.where(self.home, piece, far)
        sent = jnp.where(self.home, far, piece)
        return self.ordered(self.core, kept, self.core_swap(sent)).reshape(-1, piece.shape[1])

    def over_shards(self, value):
        if self.n_shard == 2:
            return self.ordered(self.shard, value, self.shard_swap(value))
        return lax.all_gather(value, "shard", axis=0)

    def rows_half_first(self, block):
        value = self.over_shards(self.ordered(self.half, block, self.half_swap(block)))
        return value.reshape(-1, block.shape[1])

    def rows_shard_first(self, block):
        value = self.over_shards(block)
        value = self.ordered(self.half, value, self.half_swap(value), 1)
        return value.reshape(-1, block.shape[1])


    def split_rows(self, value):
        rows, width = value.shape
        return value.reshape(self.n_shard, 2, rows // (2 * self.n_shard), width)

    def half_step(self, value, axis):
        sent = lax.dynamic_index_in_dim(value, 1 - self.half, axis, False).astype(LOW)
        kept = lax.dynamic_index_in_dim(value, self.half, axis, False)
        return kept, self.half_swap(sent), sent

    def shard_step(self, value):
        if self.n_shard == 2:
            sent = lax.dynamic_index_in_dim(value, 1 - self.shard, 0, False).astype(LOW)
            kept = lax.dynamic_index_in_dim(value, self.shard, 0, False)
            return kept, self.shard_swap(sent), sent
        kept = lax.psum_scatter(value, "shard", scatter_dimension=0, tiled=False)
        return kept, jnp.zeros_like(kept, LOW), kept

    def block_step(self, value):
        pieces = value.reshape(2, -1, value.shape[1])
        sent = lax.dynamic_index_in_dim(pieces, 1 - self.core, 0, False).astype(LOW)
        kept = lax.dynamic_index_in_dim(pieces, self.core, 0, False)
        got = self.core_swap(sent).astype(SINGLE)
        sent = jnp.where(self.home, got, kept).astype(LOW)
        return jnp.where(self.home, kept, got), self.tp_swap(sent, 2), sent

    def tp_all(self, pair, arriving):
        value = self.ordered(self.tp % 2, pair, arriving, 1)
        return value.reshape(4, *pair.shape[1:])

    def chip_total(self, value):
        value = value + self.core_swap(value)
        value = value + self.half_swap(value)
        if self.n_shard == 2:
            return value + self.shard_swap(value)
        return lax.psum(value, "shard")


def added(step, *gates):
    kept, arriving = step[:2]
    return kept + after(arriving, *gates).astype(SINGLE)


def interleaved(first, second, width):
    parts = []
    for start in range(0, first.shape[1], width):
        parts += [first[:, start : start + width], second[:, start : start + width]]
    return jnp.concatenate(parts, 1)


def shards(
    tokens,
    lengths,
    first_gain,
    entry_weight,
    entry_bias,
    exit_weight,
    exit_bias,
    second_gain,
    hidden_weight,
    hidden_bias,
    return_weight,
    return_bias,
    cotangent,
):
    place = Place()
    local, narrow = tokens.shape[1:]
    part = entry_weight.shape[1]
    head_width = entry_weight.shape[2]
    units = hidden_weight.shape[1]

    width = 2 * head_width

    piece_a = jnp.concatenate([entry_weight[1], entry_weight[2], entry_weight[0], exit_weight.T], 1)
    piece_b = jnp.concatenate([hidden_weight, return_weight.T], 1)
    biases = jnp.concatenate([entry_bias.reshape(-1), hidden_bias])
    far_a = place.tp_swap(piece_a, 2)
    bias_mine = jnp.where(place.home, biases, place.tp_swap(biases, 2))
    bias_two = jnp.stack([bias_mine, place.tp_swap(bias_mine, 1)])
    bias_q = bias_two[:, :head_width].reshape(-1)
    bias_v = bias_two[:, head_width:width].reshape(-1)
    bias_h = bias_two[:, width:].reshape(-1)
    mine_a = place.own_block(piece_a, far_a)
    other_a = place.tp_swap(mine_a, 1)

    wide = narrow + 1
    sequence = after(place.tp, other_a)
    length = lax.dynamic_index_in_dim(lengths, sequence, 0, False)
    meta = jnp.stack([place.half, place.core, length, place.ctx]).astype(jnp.int32)
    tokens_low, cot_low = (
        lax.dynamic_index_in_dim(item, sequence, 0, False) for item in (tokens, cotangent)
    )
    stream, first_unit, first_inverse, cot_full, normed_own, own_two = prepare(
        meta, tokens_low, cot_low, first_gain.reshape(1, wide)
    )
    far_own = place.half_up(normed_own)
    all_two = jnp.concatenate([own_two, place.core_swap(own_two)], 0)
    first_normed, returned_grad = all_two[:, :wide], all_two[:, wide:]

    block_kv = interleaved(mine_a[:, :width], other_a[:, :width], head_width)
    block_qe = interleaved(mine_a[:, width:], other_a[:, width:], head_width)
    half_kv = place.ordered(place.half, block_kv, place.half_swap(block_kv))
    weight_kv = place.over_shards(half_kv).reshape(-1, 2 * width)
    weight_qe = place.rows_shard_first(block_qe)
    exit_t = weight_qe[:, width:]
    weight_all = jnp.concatenate([weight_qe[:, :width], weight_kv], 1)
    piece_b = after(piece_b, other_a)
    mine_b = place.own_block(piece_b, place.tp_swap(piece_b, 2))
    other_b = place.tp_swap(mine_b, 1)

    far_own = after(far_own, weight_kv)
    far_normed = jnp.concatenate([far_own, place.core_swap(far_own)], 0)
    bias_all = jnp.concatenate([bias_q, jnp.zeros_like(bias_v), bias_v])
    block_h = jnp.concatenate([mine_b[:, :units], other_b[:, :units]], 1)
    block_r = jnp.concatenate([mine_b[:, units:], other_b[:, units:]], 1)
    block_h, block_r = after((block_h, block_r), weight_kv, weight_qe)
    half_h = place.ordered(place.half, block_h, place.half_swap(block_h))
    shard_r = place.over_shards(block_r)
    if place.n_shard == 2:
        last_h = place.shard_swap(half_h)
        hidden_full = place.ordered(place.shard, half_h, last_h)
    else:
        last_h = hidden_full = lax.all_gather(half_h, "shard")
    hidden_full = hidden_full.reshape(-1, 2 * units)
    last_r = place.half_swap(shard_r)
    return_t = place.ordered(place.half, shard_r, last_r, 1)
    return_t = return_t.reshape(-1, 2 * units)
    near = (dot(first_normed, weight_all) + bias_all).astype(LOW)
    far_kv = (dot(far_normed, weight_kv) + bias_all[width:]).astype(LOW)
    attended, logs = attend(meta, width, near, after(far_kv, half_h, shard_r))

    def joined(product, left, weight):
        sent = product(left[local:], weight).astype(LOW)
        return product(left[:local], weight), place.core_swap(sent)

    branch = added(joined(dot_nt, attended, exit_t), last_h, last_r) + exit_bias
    middle = stream + branch - row_mean(branch)
    second_inverse = lax.rsqrt(row_mean(middle * middle) + EPSILON)
    second_unit = middle * second_inverse
    second_own = (second_unit * second_gain).astype(LOW)
    second_normed = jnp.concatenate([second_own, place.core_swap(second_own)], 0)
    hidden = dot(second_normed, hidden_full) + bias_h
    activated, gelu_pull = jax.vjp(
        lambda values_in: jax.nn.gelu(values_in, approximate=True), hidden
    )
    activated_low = activated.astype(LOW)
    hidden_grad = gelu_pull(dot(returned_grad, return_t))[0].astype(LOW)

    returned_step = joined(dot_nt, activated_low, return_t)
    second_step = joined(dot_nt, after(hidden_grad, returned_step[0]), hidden_full)
    returned = added(returned_step, second_step[0]) + return_bias
    full_stream = middle + returned - row_mean(returned)
    result_own = full_stream.astype(LOW)
    result_far = place.tp_swap(result_own, 2)
    second_grad = added(second_step, result_own)

    second_scaled = second_grad * second_gain
    middle_grad = cot_full + second_inverse * (
        second_scaled - second_unit * row_mean(second_scaled * second_unit)
    )
    branch_own = (middle_grad - row_mean(middle_grad)).astype(LOW)
    branch_other = place.core_swap(branch_own)

    hidden_weight_grad = dot_tn(after(second_normed, branch_own), hidden_grad)
    return_weight_grad = dot_tn(returned_grad, after(activated_low, branch_own))
    step_h = place.half_step(place.split_rows(hidden_weight_grad), 1)
    step_r = place.shard_step(place.split_rows(return_weight_grad))

    branch_other = after(branch_other, step_h[2], step_r[2])
    branch_grad = jnp.concatenate([branch_own, branch_other], 0)
    attended_grad = dot(branch_grad, exit_t).astype(LOW)
    far_dkv, inner, mixed = attend_far_back(
        meta, width, near, far_kv, attended_grad, attended, logs
    )
    far_step = joined(dot_nt, far_dkv, weight_kv)
    exit_weight_grad = dot_tn(after(branch_grad, far_step[0]), attended)
    far_sum = added(far_step, exit_weight_grad).astype(LOW)
    far_grad = place.half_down(far_sum)
    result_pair = place.ordered(place.tp // 2, result_own, after(result_far, exit_weight_grad))
    result_near = place.tp_swap(result_pair, 1)
    mixed = after(mixed, far_sum, result_pair)
    grads = attend_near_back(meta, width, near, attended_grad, logs, inner, mixed)
    sent = dot_nt(grads[local:], weight_all).astype(LOW)
    kept = dot_nt(grads[:local], weight_all)
    sent = after(sent, result_near, far_grad)
    step_h = place.shard_step(added(step_h, kept))
    step_r = place.half_step(added(step_r, kept), 0)
    first_grad = added((kept, place.core_swap(sent)), step_h[2], step_r[2]) + far_grad.astype(SINGLE)
    first_scaled = first_grad * first_gain
    stream_grad = middle_grad + first_inverse * (
        first_scaled - first_unit * row_mean(first_scaled * first_unit)
    )
    tokens_rows = (stream_grad - stream_grad[:, narrow:]).astype(LOW)
    tokens_far = place.tp_swap(tokens_rows, 2)

    normed_late = after(first_normed, tokens_rows)
    grads = after(grads, tokens_rows)
    query_weight_grad = dot_tn(normed_late, grads[:, :width])
    kv_weight_grad = dot_tn(normed_late, grads[:, width:]) + dot_tn(
        after(far_normed, tokens_rows), far_dkv
    )
    sum_h, sum_r = added(step_h, kv_weight_grad), added(step_r, kv_weight_grad)
    mlp_sent = jnp.concatenate([sum_h[:, units:], sum_r[:, units:]], 1).astype(LOW)
    mlp = (jnp.concatenate([sum_h[:, :units], sum_r[:, :units]], 1), place.tp_swap(mlp_sent, 1))
    query_exit_grad = jnp.concatenate([query_weight_grad, exit_weight_grad], 1)
    step_qe = place.shard_step(place.split_rows(query_exit_grad))
    step_kv = place.half_step(place.split_rows(kv_weight_grad), 1)
    tokens_pair = place.ordered(
        place.tp // 2, tokens_rows, after(tokens_far, step_kv[2], step_qe[2])
    )
    tokens_near = place.tp_swap(tokens_pair, 1)
    mlp = place.block_step(added(mlp, tokens_pair))
    mlp_first = mlp[2]
    step_qe = place.half_step(added(step_qe, mlp_first), 0)
    step_kv = place.shard_step(added(step_kv, mlp_first))
    sums = jnp.concatenate([added(step_qe), added(step_kv)], 1)
    sums = [
        jnp.concatenate(
            [sums[:, at * width + low : at * width + low + head_width] for at in range(4)], 1
        )
        for low in (0, head_width)
    ]
    heads = added((sums[0], place.tp_swap(sums[1].astype(LOW), 1)), tokens_near)
    heads_sum = heads
    heads = place.block_step(heads)
    result = place.tp_all(result_pair, after(result_near, tokens_pair))[:, :, :narrow]
    mlp, heads = added(mlp, heads[0]), added(heads)
    tokens_grad = place.tp_all(tokens_pair, tokens_near)[:, :, :narrow]
    at = lambda index: heads[:, index * head_width : (index + 1) * head_width]
    entry_grad = jnp.stack([at(0), at(2), at(3)])
    exit_grad = at(1).T
    hidden_out = mlp[:, :units]
    return_out = mlp[:, units:].T

    return_bias_grad = jnp.sum(own_two[:, wide:].astype(SINGLE), 0)
    exit_bias_grad = jnp.sum(branch_own.astype(SINGLE), 0)
    first_gain_grad = jnp.sum(first_grad * first_unit, 0)
    second_gain_grad = jnp.sum(second_grad * second_unit, 0)
    query_sum = jnp.sum(grads[:, :width].astype(SINGLE), 0).reshape(2, head_width)
    value_sum = jnp.sum(grads[:, 2 * width :].astype(SINGLE), 0)
    value_sum = (value_sum + jnp.sum(far_dkv[:, width:].astype(SINGLE), 0)).reshape(2, head_width)
    hidden_sum = jnp.sum(hidden_grad.astype(SINGLE), 0).reshape(2, units)
    blocks = jnp.concatenate([query_sum, value_sum, hidden_sum], 1)
    first_id = jnp.where(place.home, place.tp, place.tp ^ 2)
    slots = []
    for slot in range(4):
        slots.append(
            jnp.where(first_id == slot, blocks[0], 0.0)
            + jnp.where(first_id == (slot ^ 1), blocks[1], 0.0)
        )
    pieces = [first_gain_grad, exit_bias_grad, second_gain_grad, return_bias_grad] + slots
    pieces = after(pieces, tokens_pair, mlp_sent)
    vectors = place.chip_total(after(jnp.concatenate(pieces), mlp_first))
    vectors = vectors + after(place.tp_swap(vectors, 1), heads_sum)
    vectors = vectors + place.tp_swap(vectors, 2)
    own = lax.dynamic_index_in_dim(vectors[4 * wide :].reshape(4, -1), place.tp, 0, False)
    return (
        result,
        tokens_grad,
        vectors[:wide],
        entry_grad,
        own[:width].reshape(2, head_width),
        exit_grad,
        vectors[wide : 2 * wide],
        vectors[2 * wide : 3 * wide],
        hidden_out,
        own[width:],
        return_out,
        vectors[3 * wide : 4 * wide],
    )


def solution(mesh):
    return jax.shard_map(
        shards,
        mesh=mesh,
        in_specs=(
            P("shard", "ctx", None),
            P("shard"),
            P(),
            P(None, ("shard", "ctx"), "tp"),
            P(None, "tp"),
            P("tp", ("shard", "ctx")),
            P(),
            P(),
            P(("shard", "ctx"), "tp"),
            P("tp"),
            P("tp", ("shard", "ctx")),
            P(),
            P("shard", "ctx", None),
        ),
        out_specs=(
            P("shard", "ctx", None),
            P("shard", "ctx", None),
            P(),
            P(None, ("shard", "ctx"), "tp"),
            P(None, "tp"),
            P("tp", ("shard", "ctx")),
            P(),
            P(),
            P(("shard", "ctx"), "tp"),
            P("tp"),
            P("tp", ("shard", "ctx")),
            P(),
        ),
        check_vma=False,
    )
```

profile of v0, /device:TPU:0, one launch (start us, length us, event | category | flops | bytes accessed | tf_op | source)
XLA Modules:
  0.0 303.3 jit_solution(7823179939460696288)
XLA Ops:
  2.1 4.1 %collective-permute-start.8 = (f32[1152]{0:T(1024)S(1)}, f32[1152]{0:T(1024)S(1)}, u32[]{:S(2)}, u32[]{:S(2)}) collective-permute-start(f32[1152]{0:T(1024)S(1)} %constant_dynamic-update-slice_fusion.13), channel_id=1, source_target_pairs={{0,2},{1,3},{2,0},{3,1},{4,6},{5,7},{6,4},{7,5},{8,10},{9,11},{10,... | collective-permute-start | bytes 13832 | tf_op jit(solution)/shard_map/ppermute | solution.py:284
  8.2 1.9 collective-permute-start.9
  10.0 7.4 %collective-permute-done = bf16[96,768]{1,0:T(8,128)(2,1)S(1)} collective-permute-done((bf16[96,768]{1,0:T(8,128)(2,1)S(1)}, bf16[96,768]{1,0:T(8,128)(2,1)S(1)}, u32[]{:S(2)}, u32[]{:S(2)}) %collective-permute-start) | collective-permute-done | bytes 147488 | tf_op jit(solution)/shard_map/ppermute | solution.py:284
  21.2 8.6 %collective-permute-done.2 = bf16[192,768]{1,0:T(8,128)(2,1)S(1)} collective-permute-done((bf16[192,768]{1,0:T(8,128)(2,1)S(1)}, bf16[192,768]{1,0:T(8,128)(2,1)S(1)}, u32[]{:S(2)}, u32[]{:S(2)}) %collective-permute-start.2) | collective-permute-done | bytes 294944 | tf_op jit(solution)/shard_map/ppermute | solution.py:284
  32.6 1.6 collective-permute-start.6
  34.8 3.5 %constant_dynamic-slice_fusion.1 = (bf16[1,256,767]{1,0,2:T(2,128)(2,1)S(1)}, bf16[1,256,767]{1,0,2:T(2,128)(2,1)S(1)}) fusion(bf16[4,256,767]{1,0,2:T(4,128)(2,1)} %param.25, s32[]{:T(128)S(6)} %select_n.338, bf16[4,256,767]{1,0,2:T(4,128)(2,1)} %param.13), kind=kLoop, calls=%fused_computation.197 | loop fusion | bytes 1570820 | tf_op jit(solution)/shard_map/jit(dynamic_index_in_dim)/dynamic_slice | solution.py:401
  38.3 1.8 copy.35
  40.1 1.8 copy.34
  43.1 3.9 %prepare.1 = (f32[256,768]{1,0:T(8,128)}, f32[256,768]{1,0:T(8,128)}, f32[256,1]{1,0:T(8,128)}, f32[256,768]{1,0:T(8,128)}, bf16[256,768]{1,0:T(8,128)(2,1)}, /*index=5*/bf16[256,1536]{1,0:T(8,128)(2,1)}) custom-call(s32[4]{0:T(128)} %pad_add_fusion.meta, bf16[256,767]{1,0:T(8,128)(2,1)} %bitcast.204, bf16[256,767]{1,0:T(8,128)(2,1)} %bitcast.203, ...), custom_call_target="tpu_custom_call" | custom-call | flops 3932160 | bytes 3932160 | tf_op jit(solution)/shard_map/prepare/pallas_call | solution.py:96
  47.0 2.6 collective-permute-start.10
  52.7 1.8 collective-permute-start.14
  54.6 15.3 %collective-permute-done.5 = bf16[2,192,768]{2,1,0:T(8,128)(2,1)S(1)} collective-permute-done((bf16[2,192,768]{2,1,0:T(8,128)(2,1)S(1)}, bf16[2,192,768]{2,1,0:T(8,128)(2,1)S(1)}, u32[]{:S(2)}, u32[]{:S(2)}) %collective-permute-start.5) | collective-permute-done | bytes 589856 | tf_op jit(solution)/shard_map/ppermute | solution.py:272
  70.5 2.5 collective-permute-start.15
  74.2 2.2 fusion.7.q_ref.k_ref.v_ref
  77.0 7.8 %collective-permute-done.15 = bf16[192,1536]{1,0:T(8,128)(2,1)S(1)} collective-permute-done((bf16[192,1536]{1,0:T(8,128)(2,1)S(1)}, bf16[192,1536]{1,0:T(8,128)(2,1)S(1)}, u32[]{:S(2)}, u32[]{:S(2)}) %collective-permute-start.15) | collective-permute-done | bytes 589856 | tf_op jit(solution)/shard_map/ppermute | solution.py:272
  86.6 6.1 %collective-permute-done.16 = bf16[192,1536]{1,0:T(8,128)(2,1)S(1)} collective-permute-done((bf16[192,1536]{1,0:T(8,128)(2,1)S(1)}, bf16[192,1536]{1,0:T(8,128)(2,1)S(1)}, u32[]{:S(2)}, u32[]{:S(2)}) %collective-permute-start.16) | collective-permute-done | bytes 589856 | tf_op jit(solution)/shard_map/ppermute | solution.py:281
  96.5 1.7 add_convert_fusion.kf_ref.vf_ref.k_ref.v_ref
  98.1 13.3 %attend.1 = (bf16[512,384]{1,0:T(8,128)(2,1)}, f32[3,2,512]{2,1,0:T(2,128)}) custom-call(s32[4]{0:T(128)} %pad_add_fusion.meta, bf16[512,1152]{1,0:T(8,128)(2,1)} %fusion.7.q_ref.k_ref.v_ref, bf16[512,1152]{1,0:T(8,128)(2,1)} %fusion.7.q_ref.k_ref.v_ref, bf16[512,1152]{1,0:T(8,128)(2,1)} %fusion.7.q_ref.k_ref.v_ref, ...), custom_call_target="tpu_custom_call" | custom-call | flops 805306368 | bytes 3145728 | tf_op jit(solution)/shard_map/attend/pallas_call | solution.py:204
  111.4 2.4 convolution_convert_fusion.5
  116.8 2.9 collective-permute-done.19
  122.8 1.6 select_bitcast_fusion.3
  127.5 2.0 multiply_convert_fusion
  132.1 3.9 %convert_reduce_fusion = (f32[1536]{0:T(1024)S(1)}, bf16[512,1536]{1,0:T(8,128)(2,1)}) fusion(f32[512,1536]{1,0:T(8,128)S(1)} %get-tuple-element.232, bf16[768,1536]{1,0:T(8,128)(2,1)S(1)} %bitcast.198, bf16[512,1536]{1,0:T(8,128)(2,1)S(1)} %copy-done.19), kind=kOutput, calls=%fused_computation.11 | convolution fusion | flops 1225259520 | bytes 7870464 | tf_op jit(solution)/shard_map/dot_general | solution.py:24
  136.6 2.9 convolution_convert_fusion.3
  145.6 2.5 collective-permute-start.22
  158.1 10.1 %attend_far_back.1 = (bf16[512,768]{1,0:T(8,128)(2,1)}, f32[3,2,512]{2,1,0:T(2,128)}, f32[3,128,512]{2,1,0:T(8,128)}) custom-call(s32[4]{0:T(128)} %pad_add_fusion.meta, bf16[512,1152]{1,0:T(8,128)(2,1)} %fusion.7.q_ref.k_ref.v_ref, bf16[512,768]{1,0:T(8,128)(2,1)} %add_convert_fusion.kf_ref.vf_ref.k_ref.v_ref, ...), custom_call_target="tpu_custom_call" | custom-call | flops 805306368 | bytes 3145728 | tf_op jit(solution)/shard_map/attend_far_back/pallas_call | solution.py:204
  176.6 11.0 %attend_near_back.1 = bf16[512,1152]{1,0:T(8,128)(2,1)} custom-call(s32[4]{0:T(128)} %pad_add_fusion.meta, bf16[512,1152]{1,0:T(8,128)(2,1)} %fusion.7.q_ref.k_ref.v_ref, bf16[512,1152]{1,0:T(8,128)(2,1)} %fusion.7.q_ref.k_ref.v_ref, bf16[512,1152]{1,0:T(8,128)(2,1)} %fusion.7.q_ref.k_ref.v_ref, bf16[512,384]{1,0:T(8,128)(2,1)} %convolution_convert_fusion.2.grad_ref, ...), custom_call_target="tpu_custom_call" | custom-call | flops 805306368 | bytes 3145728 | tf_op jit(solution)/shard_map/attend_near_back/pallas_call | solution.py:204
  187.6 2.1 convolution_convert_fusion
  189.8 1.8 fusion.31
  191.6 2.3 bitcast_add_fusion
  195.0 2.7 collective-permute-start.34
  197.8 1.7 bitcast_add_fusion.1
  208.1 1.9 fusion.13
  212.0 3.2 %pad_maximum_fusion.2 = f32[768,768]{0,1:T(8,128)} fusion(f32[768,384]{0,1:T(8,128)} %fusion.77, f32[768,384]{0,1:T(8,128)} %fusion.42), kind=kLoop, calls=%fused_computation.16 | loop fusion | flops 589824 | bytes 4718592 | tf_op jit(solution)/shard_map/concatenate | solution.py:515
  215.2 3.0 %copy.39 = f32[768,768]{1,0:T(8,128)} copy(f32[768,768]{0,1:T(8,128)} %pad_maximum_fusion.2) | data formatting | bytes 4718592 | tf_op jit(solution)/shard_map/concatenate | solution.py:515
  218.3 2.2 fusion.28
  221.2 2.0 convolution_add_fusion.2
  228.7 1.6 bitcast_add_fusion.5
  238.1 9.6 %collective-permute-done.35 = bf16[192,1536]{1,0:T(8,128)(2,1)S(1)} collective-permute-done((bf16[192,1536]{1,0:T(8,128)(2,1)S(1)}, bf16[192,1536]{1,0:T(8,128)(2,1)S(1)}, u32[]{:S(2)}, u32[]{:S(2)}) %collective-permute-start.35) | collective-permute-done | bytes 589856 | tf_op jit(solution)/shard_map/ppermute | solution.py:284
  249.9 3.9 %copy.42 = bf16[4,256,767]{1,0,2:T(4,128)(2,1)} copy(bf16[4,256,767]{2,1,0:T(8,128)(2,1)} %bitcast.175) | data formatting | bytes 3141632
  255.1 1.7 fusion.24
  256.9 1.6 collective-permute-start.49
  261.2 1.9 collective-permute-start.38
  266.6 1.9 collective-permute-start.42
  268.5 4.4 %collective-permute-done.39 = f32[7680]{0:T(1024)S(1)} collective-permute-done((f32[7680]{0:T(1024)S(1)}, f32[7680]{0:T(1024)S(1)}, u32[]{:S(2)}, u32[]{:S(2)}) %collective-permute-start.39) | collective-permute-done | bytes 30752 | tf_op jit(solution)/shard_map/ppermute | solution.py:281
  276.9 7.2 %collective-permute-done.45 = bf16[192,768]{1,0:T(8,128)(2,1)S(1)} collective-permute-done((bf16[192,768]{1,0:T(8,128)(2,1)S(1)}, bf16[192,768]{1,0:T(8,128)(2,1)S(1)}, u32[]{:S(2)}, u32[]{:S(2)}) %collective-permute-start.45) | collective-permute-done | bytes 294944 | tf_op jit(solution)/shard_map/ppermute | solution.py:284
  286.3 2.2 copy.43
  293.3 6.4 %collective-permute-done.48 = bf16[96,768]{1,0:T(8,128)(2,1)S(1)} collective-permute-done((bf16[96,768]{1,0:T(8,128)(2,1)S(1)}, bf16[96,768]{1,0:T(8,128)(2,1)S(1)}, u32[]{:S(2)}, u32[]{:S(2)}) %collective-permute-start.48) | collective-permute-done | bytes 147488 | tf_op jit(solution)/shard_map/ppermute | solution.py:284
  (397 shorter events, 108.2 us)
Async XLA Ops:
  2.1 6.0 %collective-permute-start.8 = (f32[1152]{0:T(1024)S(1)}, f32[1152]{0:T(1024)S(1)}, u32[]{:S(2)}, u32[]{:S(2)}) collective-permute-start(f32[1152]{0:T(1024)S(1)} %constant_dynamic-update-slice_fusion.13), channel_id=1, source_target_pairs={{0,2},{1,3},{2,0},{3,1},{4,6},{5,7},{6,4},{7,5},{8,10},{9,11},{10,... | collective-permute-start | bytes 13832 | tf_op jit(solution)/shard_map/ppermute | solution.py:284
  8.1 9.4 %collective-permute-start = (bf16[96,768]{1,0:T(8,128)(2,1)S(1)}, bf16[96,768]{1,0:T(8,128)(2,1)S(1)}, u32[]{:S(2)}, u32[]{:S(2)}) collective-permute-start(bf16[96,768]{1,0:T(8,128)(2,1)S(1)} %pad_maximum_fusion.29), channel_id=1, source_target_pairs={{0,2},{1,3},{2,0},{3,1},{4,6},{5,7},{6,4},{7,5},{8,10},{9,11},{10,... | collective-permute-start | bytes 442376 | tf_op jit(solution)/shard_map/ppermute | solution.py:284
  8.2 11.1 %collective-permute-start.9 = (f32[1152]{0:T(1024)S(1)}, f32[1152]{0:T(1024)S(1)}, u32[]{:S(2)}, u32[]{:S(2)}) collective-permute-start(f32[1152]{0:T(1024)S(1)} %broadcast_select_fusion.12), channel_id=1, source_target_pairs={{0,1},{1,0},{2,3},{3,2},{4,5},{5,4},{6,7},{7,6},{8,9},{9,8},{10,11... | collective-permute-start | bytes 13832 | tf_op jit(solution)/shard_map/ppermute | solution.py:284
  20.4 9.5 %collective-permute-start.2 = (bf16[192,768]{1,0:T(8,128)(2,1)S(1)}, bf16[192,768]{1,0:T(8,128)(2,1)S(1)}, u32[]{:S(2)}, u32[]{:S(2)}) collective-permute-start(bf16[192,768]{1,0:T(8,128)(2,1)S(1)} %bitcast.201), channel_id=1, source_target_pairs={{0,1},{1,0},{2,3},{3,2},{4,5},{5,4},{6,7},{7,6},{8,9},{9,8},{10,11... | collective-permute-start | bytes 884744 | tf_op jit(solution)/shard_map/ppermute | solution.py:284
  29.9 19.8 %collective-permute-start.12 = (bf16[96,1536]{1,0:T(8,128)(2,1)S(1)}, bf16[96,1536]{1,0:T(8,128)(2,1)S(1)}, u32[]{:S(2)}, u32[]{:S(2)}) collective-permute-start(bf16[96,1536]{1,0:T(8,128)(2,1)S(1)} %pad_maximum_fusion.26), channel_id=1, source_target_pairs={{0,2},{1,3},{2,0},{3,1},{4,6},{5,7},{6,4},{7,5},{8,10},{9,11},{10,... | collective-permute-start | bytes 884744 | tf_op jit(solution)/shard_map/ppermute | solution.py:284
  30.9 19.4 %collective-permute-start.4 = (bf16[192,768]{1,0:T(8,128)(2,1)}, bf16[192,768]{1,0:T(8,128)(2,1)}, u32[]{:S(2)}, u32[]{:S(2)}) collective-permute-start(bf16[192,768]{1,0:T(8,128)(2,1)} %pad_maximum_fusion.24), channel_id=1, source_target_pairs={{0,16},{16,0},{1,17},{17,1},{2,18},{18,2},{3,19},{19,3},{4,20},{20... | collective-permute-start | bytes 884744 | tf_op jit(solution)/shard_map/ppermute | solution.py:281
  32.6 19.0 %collective-permute-start.6 = (bf16[192,768]{1,0:T(8,128)(2,1)S(1)}, bf16[192,768]{1,0:T(8,128)(2,1)S(1)}, u32[]{:S(2)}, u32[]{:S(2)}) collective-permute-start(bf16[192,768]{1,0:T(8,128)(2,1)S(1)} %pad_maximum_fusion.25), channel_id=1, source_target_pairs={{0,8},{4,12},{8,0},{12,4},{1,9},{5,13},{9,1},{13,5},{2,10},{6,14},... | collective-permute-start | bytes 884744 | tf_op jit(solution)/shard_map/ppermute | solution.py:272
  47.0 26.3 %collective-permute-start.10 = (bf16[256,768]{1,0:T(8,128)(2,1)}, bf16[256,768]{1,0:T(8,128)(2,1)S(1)}, u32[]{:S(2)}, u32[]{:S(2)}) collective-permute-start(bf16[256,768]{1,0:T(8,128)(2,1)} %get-tuple-element.69), channel_id=1, source_target_pairs={{0,8},{4,12},{1,9},{5,13},{2,10},{6,14},{3,11},{7,15},{16,24},{20,... | collective-permute-start | bytes 1179656 | tf_op jit(solution)/shard_map/ppermute | solution.py:275
  49.6 23.6 %collective-permute-start.3 = (bf16[256,1536]{1,0:T(8,128)(2,1)}, bf16[256,1536]{1,0:T(8,128)(2,1)S(1)}, u32[]{:S(2)}, u32[]{:S(2)}) collective-permute-start(bf16[256,1536]{1,0:T(8,128)(2,1)} %get-tuple-element.68), channel_id=1, source_target_pairs={{0,4},{4,0},{8,12},{12,8},{1,5},{5,1},{9,13},{13,9},{2,6},{6,2},{1... | collective-permute-start | bytes 2359304 | tf_op jit(solution)/shard_map/ppermute | solution.py:269
  49.7 2.9 collective-permute-start.13
  51.5 18.3 %collective-permute-start.5 = (bf16[2,192,768]{2,1,0:T(8,128)(2,1)S(1)}, bf16[2,192,768]{2,1,0:T(8,128)(2,1)S(1)}, u32[]{:S(2)}, u32[]{:S(2)}) collective-permute-start(bf16[2,192,768]{2,1,0:T(8,128)(2,1)S(1)} %pad_maximum_fusion.14), channel_id=1, source_target_pairs={{0,8},{4,12},{8,0},{12,4},{1,9},{5,13},{9,1},{13,5},{2,10},{6,14},... | collective-permute-start | bytes 1769480 | tf_op jit(solution)/shard_map/ppermute | solution.py:272
  51.9 18.2 %collective-permute-start.7 = (bf16[2,192,768]{2,1,0:T(8,128)(2,1)S(1)}, bf16[2,192,768]{2,1,0:T(8,128)(2,1)S(1)}, u32[]{:S(2)}, u32[]{:S(2)}) collective-permute-start(bf16[2,192,768]{2,1,0:T(8,128)(2,1)S(1)} %pad_maximum_fusion.15), channel_id=1, source_target_pairs={{0,16},{16,0},{1,17},{17,1},{2,18},{18,2},{3,19},{19,3},{4,20},{20... | collective-permute-start | bytes 1769480 | tf_op jit(solution)/shard_map/ppermute | solution.py:281
  52.7 17.7 %collective-permute-start.14 = (bf16[192,1536]{1,0:T(8,128)(2,1)S(1)}, bf16[192,1536]{1,0:T(8,128)(2,1)S(1)}, u32[]{:S(2)}, u32[]{:S(2)}) collective-permute-start(bf16[192,1536]{1,0:T(8,128)(2,1)S(1)} %bitcast.199), channel_id=1, source_target_pairs={{0,1},{1,0},{2,3},{3,2},{4,5},{5,4},{6,7},{7,6},{8,9},{9,8},{10,11... | collective-permute-start | bytes 1769480 | tf_op jit(solution)/shard_map/ppermute | solution.py:284
  70.5 14.3 %collective-permute-start.15 = (bf16[192,1536]{1,0:T(8,128)(2,1)S(1)}, bf16[192,1536]{1,0:T(8,128)(2,1)S(1)}, u32[]{:S(2)}, u32[]{:S(2)}) collective-permute-start(bf16[192,1536]{1,0:T(8,128)(2,1)S(1)} %get-tuple-element.72), channel_id=1, source_target_pairs={{0,8},{4,12},{8,0},{12,4},{1,9},{5,13},{9,1},{13,5},{2,10},{6,14},... | collective-permute-start | bytes 1769480 | tf_op jit(solution)/shard_map/ppermute | solution.py:272
  73.3 22.1 %collective-permute-start.11 = (bf16[256,768]{1,0:T(8,128)(2,1)S(1)}, bf16[256,768]{1,0:T(8,128)(2,1)S(1)}, u32[]{:S(2)}, u32[]{:S(2)}) collective-permute-start(bf16[256,768]{1,0:T(8,128)(2,1)S(1)} %collective-permute-done.10), channel_id=1, source_target_pairs={{0,4},{4,0},{8,12},{12,8},{1,5},{5,1},{9,13},{13,9},{2,6},{6,2},{1... | collective-permute-start | bytes 1179656 | tf_op jit(solution)/shard_map/ppermute | solution.py:269
  76.5 16.2 %collective-permute-start.16 = (bf16[192,1536]{1,0:T(8,128)(2,1)S(1)}, bf16[192,1536]{1,0:T(8,128)(2,1)S(1)}, u32[]{:S(2)}, u32[]{:S(2)}) collective-permute-start(bf16[192,1536]{1,0:T(8,128)(2,1)S(1)} %get-tuple-element.73), channel_id=1, source_target_pairs={{0,16},{16,0},{1,17},{17,1},{2,18},{18,2},{3,19},{19,3},{4,20},{20... | collective-permute-start | bytes 1769480 | tf_op jit(solution)/shard_map/ppermute | solution.py:281
  86.0 30.7 %collective-permute-start.18 = (bf16[2,192,1536]{2,1,0:T(8,128)(2,1)}, bf16[2,192,1536]{2,1,0:T(8,128)(2,1)}, u32[]{:S(2)}, u32[]{:S(2)}) collective-permute-start(bf16[2,192,1536]{2,1,0:T(8,128)(2,1)} %pad_maximum_fusion.8), channel_id=1, source_target_pairs={{0,16},{16,0},{1,17},{17,1},{2,18},{18,2},{3,19},{19,3},{4,20},{20... | collective-permute-start | bytes 3538952 | tf_op jit(solution)/shard_map/ppermute | solution.py:281
  94.0 25.7 %collective-permute-start.19 = (bf16[2,192,1536]{2,1,0:T(8,128)(2,1)}, bf16[2,192,1536]{2,1,0:T(8,128)(2,1)}, u32[]{:S(2)}, u32[]{:S(2)}) collective-permute-start(bf16[2,192,1536]{2,1,0:T(8,128)(2,1)} %pad_maximum_fusion.9), channel_id=1, source_target_pairs={{0,8},{4,12},{8,0},{12,4},{1,9},{5,13},{9,1},{13,5},{2,10},{6,14},... | collective-permute-start | bytes 3538952 | tf_op jit(solution)/shard_map/ppermute | solution.py:272
  113.8 2.7 collective-permute-start.17
  122.7 3.6 %collective-permute-start.20 = (bf16[256,768]{1,0:T(8,128)(2,1)S(1)}, bf16[256,768]{1,0:T(8,128)(2,1)S(1)}, u32[]{:S(2)}, u32[]{:S(2)}) collective-permute-start(bf16[256,768]{1,0:T(8,128)(2,1)S(1)} %multiply_convert_fusion.1), channel_id=1, source_target_pairs={{0,4},{4,0},{8,12},{12,8},{1,5},{5,1},{9,13},{13,9},{2,6},{6,2},{1... | collective-permute-start | bytes 1179656 | tf_op jit(solution)/shard_map/ppermute | solution.py:269
  139.5 3.5 %collective-permute-start.23 = (bf16[256,768]{1,0:T(8,128)(2,1)S(1)}, bf16[256,768]{1,0:T(8,128)(2,1)S(1)}, u32[]{:S(2)}, u32[]{:S(2)}) collective-permute-start(bf16[256,768]{1,0:T(8,128)(2,1)S(1)} %convolution_convert_fusion.3), channel_id=1, source_target_pairs={{0,4},{4,0},{8,12},{12,8},{1,5},{5,1},{9,13},{13,9},{2,6},{6,2},{1... | collective-permute-start | bytes 1179656 | tf_op jit(solution)/shard_map/ppermute | solution.py:269
  145.3 11.5 %collective-permute-start.24 = (bf16[256,768]{1,0:T(8,128)(2,1)S(1)}, bf16[256,768]{1,0:T(8,128)(2,1)S(1)}, u32[]{:S(2)}, u32[]{:S(2)}) collective-permute-start(bf16[256,768]{1,0:T(8,128)(2,1)S(1)} %get-tuple-element.161), channel_id=1, source_target_pairs={{0,4},{4,0},{8,12},{12,8},{1,5},{5,1},{9,13},{13,9},{2,6},{6,2},{1... | collective-permute-start | bytes 1179656 | tf_op jit(solution)/shard_map/ppermute | solution.py:269
  145.6 26.9 %collective-permute-start.22 = (bf16[256,768]{1,0:T(8,128)(2,1)}, bf16[256,768]{1,0:T(8,128)(2,1)S(1)}, u32[]{:S(2)}, u32[]{:S(2)}) collective-permute-start(bf16[256,768]{1,0:T(8,128)(2,1)} %subtract_convert_fusion.2), channel_id=1, source_target_pairs={{0,2},{1,3},{2,0},{3,1},{4,6},{5,7},{6,4},{7,5},{8,10},{9,11},{10,... | collective-permute-start | bytes 1179656 | tf_op jit(solution)/shard_map/ppermute | solution.py:284
  152.1 39.5 %collective-permute-start.30 = (bf16[2,192,1536]{2,1,0:T(8,128)(2,1)}, bf16[2,192,1536]{2,1,0:T(8,128)(2,1)}, u32[]{:S(2)}, u32[]{:S(2)}) collective-permute-start(bf16[2,192,1536]{2,1,0:T(8,128)(2,1)} %fusion.9), channel_id=1, source_target_pairs={{0,16},{16,0},{1,17},{17,1},{2,18},{18,2},{3,19},{19,3},{4,20},{20... | collective-permute-start | bytes 3538952 | tf_op jit(solution)/shard_map/ppermute | solution.py:281
  155.2 42.4 %collective-permute-start.29 = (bf16[2,192,1536]{2,1,0:T(8,128)(2,1)}, bf16[2,192,1536]{2,1,0:T(8,128)(2,1)}, u32[]{:S(2)}, u32[]{:S(2)}) collective-permute-start(bf16[2,192,1536]{2,1,0:T(8,128)(2,1)} %fusion.8), channel_id=1, source_target_pairs={{0,8},{4,12},{8,0},{12,4},{1,9},{5,13},{9,1},{13,5},{2,10},{6,14},... | collective-permute-start | bytes 3538952 | tf_op jit(solution)/shard_map/ppermute | solution.py:272
  170.3 4.9 %collective-permute-start.26 = (bf16[256,768]{1,0:T(8,128)(2,1)S(1)}, bf16[256,768]{1,0:T(8,128)(2,1)S(1)}, u32[]{:S(2)}, u32[]{:S(2)}) collective-permute-start(bf16[256,768]{1,0:T(8,128)(2,1)S(1)} %convolution_convert_fusion.1), channel_id=1, source_target_pairs={{0,4},{4,0},{8,12},{12,8},{1,5},{5,1},{9,13},{13,9},{2,6},{6,2},{1... | collective-permute-start | bytes 1179656 | tf_op jit(solution)/shard_map/ppermute | solution.py:269
  174.6 23.0 %collective-permute-start.25 = (bf16[2,256,768]{2,1,0:T(8,128)(2,1)}, bf16[2,256,768]{2,1,0:T(8,128)(2,1)}, u32[]{:S(2)}, u32[]{:S(2)}) collective-permute-start(bf16[2,256,768]{2,1,0:T(8,128)(2,1)} %pad_maximum_fusion.12), channel_id=1, source_target_pairs={{0,1},{1,0},{2,3},{3,2},{4,5},{5,4},{6,7},{7,6},{8,9},{9,8},{10,11... | collective-permute-start | bytes 2359304 | tf_op jit(solution)/shard_map/ppermute | solution.py:284
  175.3 22.3 %collective-permute-start.27 = (bf16[256,768]{1,0:T(8,128)(2,1)S(1)}, bf16[256,768]{1,0:T(8,128)(2,1)S(1)}, u32[]{:S(2)}, u32[]{:S(2)}) collective-permute-start(bf16[256,768]{1,0:T(8,128)(2,1)S(1)} %add_convert_fusion.1), channel_id=1, source_target_pairs={{8,0},{12,4},{9,1},{13,5},{10,2},{14,6},{11,3},{15,7},{24,16},{28,... | collective-permute-start | bytes 1179656 | tf_op jit(solution)/shard_map/ppermute | solution.py:278
  195.0 32.1 %collective-permute-start.34 = (bf16[192,1536]{1,0:T(8,128)(2,1)}, bf16[192,1536]{1,0:T(8,128)(2,1)}, u32[]{:S(2)}, u32[]{:S(2)}) collective-permute-start(bf16[192,1536]{1,0:T(8,128)(2,1)} %fusion.27), channel_id=1, source_target_pairs={{0,8},{4,12},{8,0},{12,4},{1,9},{5,13},{9,1},{13,5},{2,10},{6,14},... | collective-permute-start | bytes 1769480 | tf_op jit(solution)/shard_map/ppermute | solution.py:272
  197.6 4.3 %collective-permute-start.28 = (bf16[256,768]{1,0:T(8,128)(2,1)S(1)}, bf16[256,768]{1,0:T(8,128)(2,1)S(1)}, u32[]{:S(2)}, u32[]{:S(2)}) collective-permute-start(bf16[256,768]{1,0:T(8,128)(2,1)S(1)} %convolution_convert_fusion), channel_id=1, source_target_pairs={{0,4},{4,0},{8,12},{12,8},{1,5},{5,1},{9,13},{13,9},{2,6},{6,2},{1... | collective-permute-start | bytes 1179656 | tf_op jit(solution)/shard_map/ppermute | solution.py:269
  200.4 28.3 %collective-permute-start.33 = (bf16[192,1536]{1,0:T(8,128)(2,1)}, bf16[192,1536]{1,0:T(8,128)(2,1)}, u32[]{:S(2)}, u32[]{:S(2)}) collective-permute-start(bf16[192,1536]{1,0:T(8,128)(2,1)} %fusion.26), channel_id=1, source_target_pairs={{0,16},{16,0},{1,17},{17,1},{2,18},{18,2},{3,19},{19,3},{4,20},{20... | collective-permute-start | bytes 1769480 | tf_op jit(solution)/shard_map/ppermute | solution.py:281
  204.4 28.1 %collective-permute-start.31 = (bf16[256,768]{1,0:T(8,128)(2,1)S(1)}, bf16[256,768]{1,0:T(8,128)(2,1)}, u32[]{:S(2)}, u32[]{:S(2)}) collective-permute-start(bf16[256,768]{1,0:T(8,128)(2,1)S(1)} %subtract_convert_fusion), channel_id=1, source_target_pairs={{0,2},{1,3},{2,0},{3,1},{4,6},{5,7},{6,4},{7,5},{8,10},{9,11},{10,... | collective-permute-start | bytes 1179656 | tf_op jit(solution)/shard_map/ppermute | solution.py:284
  220.5 38.0 %collective-permute-start.41 = (bf16[2,192,768]{2,1,0:T(8,128)(2,1)}, bf16[2,192,768]{2,1,0:T(8,128)(2,1)}, u32[]{:S(2)}, u32[]{:S(2)}) collective-permute-start(bf16[2,192,768]{2,1,0:T(8,128)(2,1)} %fusion.28), channel_id=1, source_target_pairs={{0,16},{16,0},{1,17},{17,1},{2,18},{18,2},{3,19},{19,3},{4,20},{20... | collective-permute-start | bytes 1769480 | tf_op jit(solution)/shard_map/ppermute | solution.py:281
  225.5 33.0 %collective-permute-start.43 = (bf16[2,192,768]{2,1,0:T(8,128)(2,1)}, bf16[2,192,768]{2,1,0:T(8,128)(2,1)}, u32[]{:S(2)}, u32[]{:S(2)}) collective-permute-start(bf16[2,192,768]{2,1,0:T(8,128)(2,1)} %fusion.29), channel_id=1, source_target_pairs={{0,8},{4,12},{8,0},{12,4},{1,9},{5,13},{9,1},{13,5},{2,10},{6,14},... | collective-permute-start | bytes 1769480 | tf_op jit(solution)/shard_map/ppermute | solution.py:272
  231.4 16.3 %collective-permute-start.35 = (bf16[192,1536]{1,0:T(8,128)(2,1)S(1)}, bf16[192,1536]{1,0:T(8,128)(2,1)S(1)}, u32[]{:S(2)}, u32[]{:S(2)}) collective-permute-start(bf16[192,1536]{1,0:T(8,128)(2,1)S(1)} %pad_maximum_fusion.19), channel_id=1, source_target_pairs={{0,1},{1,0},{2,3},{3,2},{4,5},{5,4},{6,7},{7,6},{8,9},{9,8},{10,11... | collective-permute-start | bytes 1769480 | tf_op jit(solution)/shard_map/ppermute | solution.py:284
  235.5 38.8 %collective-permute-start.32 = (bf16[2,256,768]{2,1,0:T(8,128)(2,1)}, bf16[2,256,768]{2,1,0:T(8,128)(2,1)}, u32[]{:S(2)}, u32[]{:S(2)}) collective-permute-start(bf16[2,256,768]{2,1,0:T(8,128)(2,1)} %pad_maximum_fusion.13), channel_id=1, source_target_pairs={{0,1},{1,0},{2,3},{3,2},{4,5},{5,4},{6,7},{7,6},{8,9},{9,8},{10,11... | collective-permute-start | bytes 2359304 | tf_op jit(solution)/shard_map/ppermute | solution.py:284
  248.6 6.5 %collective-permute-start.36 = (bf16[96,1536]{1,0:T(8,128)(2,1)}, bf16[96,1536]{1,0:T(8,128)(2,1)}, u32[]{:S(2)}, u32[]{:S(2)}) collective-permute-start(bf16[96,1536]{1,0:T(8,128)(2,1)} %fusion.45), channel_id=1, source_target_pairs={{0,4},{4,0},{8,12},{12,8},{1,5},{5,1},{9,13},{13,9},{2,6},{6,2},{1... | collective-permute-start | bytes 884744 | tf_op jit(solution)/shard_map/ppermute | solution.py:269
  256.9 42.9 %collective-permute-start.49 = (bf16[96,1536]{1,0:T(8,128)(2,1)}, bf16[96,1536]{1,0:T(8,128)(2,1)}, u32[]{:S(2)}, u32[]{:S(2)}) collective-permute-start(bf16[96,1536]{1,0:T(8,128)(2,1)} %fusion.24), channel_id=1, source_target_pairs={{0,2},{1,3},{2,0},{3,1},{4,6},{5,7},{6,4},{7,5},{8,10},{9,11},{10,... | collective-permute-start | bytes 884744 | tf_op jit(solution)/shard_map/ppermute | solution.py:284
  258.5 2.7 collective-permute-start.37
  261.2 4.0 %collective-permute-start.38 = (f32[7680]{0:T(1024)S(1)}, f32[7680]{0:T(1024)S(1)}, u32[]{:S(2)}, u32[]{:S(2)}) collective-permute-start(f32[7680]{0:T(1024)S(1)} %add.291), channel_id=1, source_target_pairs={{0,8},{4,12},{8,0},{12,4},{1,9},{5,13},{9,1},{13,5},{2,10},{6,14},... | collective-permute-start | bytes 92168 | tf_op jit(solution)/shard_map/ppermute | solution.py:272
  263.2 12.4 %collective-permute-start.44 = (bf16[192,768]{1,0:T(8,128)(2,1)S(1)}, bf16[192,768]{1,0:T(8,128)(2,1)S(1)}, u32[]{:S(2)}, u32[]{:S(2)}) collective-permute-start(bf16[192,768]{1,0:T(8,128)(2,1)S(1)} %fusion.47), channel_id=1, source_target_pairs={{0,16},{16,0},{1,17},{17,1},{2,18},{18,2},{3,19},{19,3},{4,20},{20... | collective-permute-start | bytes 884744 | tf_op jit(solution)/shard_map/ppermute | solution.py:281
  265.2 7.7 %collective-permute-start.39 = (f32[7680]{0:T(1024)S(1)}, f32[7680]{0:T(1024)S(1)}, u32[]{:S(2)}, u32[]{:S(2)}) collective-permute-start(f32[7680]{0:T(1024)S(1)} %add.292), channel_id=1, source_target_pairs={{0,16},{16,0},{1,17},{17,1},{2,18},{18,2},{3,19},{19,3},{4,20},{20... | collective-permute-start | bytes 92168 | tf_op jit(solution)/shard_map/ppermute | solution.py:281
  266.6 9.3 %collective-permute-start.42 = (bf16[192,768]{1,0:T(8,128)(2,1)S(1)}, bf16[192,768]{1,0:T(8,128)(2,1)S(1)}, u32[]{:S(2)}, u32[]{:S(2)}) collective-permute-start(bf16[192,768]{1,0:T(8,128)(2,1)S(1)} %fusion.46), channel_id=1, source_target_pairs={{0,8},{4,12},{8,0},{12,4},{1,9},{5,13},{9,1},{13,5},{2,10},{6,14},... | collective-permute-start | bytes 884744 | tf_op jit(solution)/shard_map/ppermute | solution.py:272
  272.9 11.4 %collective-permute-start.40 = (f32[7680]{0:T(1024)S(1)}, f32[7680]{0:T(1024)S(1)}, u32[]{:S(2)}, u32[]{:S(2)}) collective-permute-start(f32[7680]{0:T(1024)S(1)} %add.293), channel_id=1, source_target_pairs={{0,1},{1,0},{2,3},{3,2},{4,5},{5,4},{6,7},{7,6},{8,9},{9,8},{10,11... | collective-permute-start | bytes 92168 | tf_op jit(solution)/shard_map/ppermute | solution.py:284
  276.2 7.9 %collective-permute-start.45 = (bf16[192,768]{1,0:T(8,128)(2,1)S(1)}, bf16[192,768]{1,0:T(8,128)(2,1)S(1)}, u32[]{:S(2)}, u32[]{:S(2)}) collective-permute-start(bf16[192,768]{1,0:T(8,128)(2,1)S(1)} %pad_maximum_fusion.27), channel_id=1, source_target_pairs={{0,1},{1,0},{2,3},{3,2},{4,5},{5,4},{6,7},{7,6},{8,9},{9,8},{10,11... | collective-permute-start | bytes 884744 | tf_op jit(solution)/shard_map/ppermute | solution.py:284
  284.3 5.3 %collective-permute-start.46 = (f32[7680]{0:T(1024)S(1)}, f32[7680]{0:T(1024)}, u32[]{:S(2)}, u32[]{:S(2)}) collective-permute-start(f32[7680]{0:T(1024)S(1)} %add.299), channel_id=1, source_target_pairs={{0,2},{1,3},{2,0},{3,1},{4,6},{5,7},{6,4},{7,5},{8,10},{9,11},{10,... | collective-permute-start | bytes 92168 | tf_op jit(solution)/shard_map/ppermute | solution.py:284
  286.0 4.4 %collective-permute-start.47 = (bf16[96,768]{1,0:T(8,128)(2,1)}, bf16[96,768]{1,0:T(8,128)(2,1)S(1)}, u32[]{:S(2)}, u32[]{:S(2)}) collective-permute-start(bf16[96,768]{1,0:T(8,128)(2,1)} %fusion.50), channel_id=1, source_target_pairs={{0,4},{4,0},{8,12},{12,8},{1,5},{5,1},{9,13},{13,9},{2,6},{6,2},{1... | collective-permute-start | bytes 442376 | tf_op jit(solution)/shard_map/ppermute | solution.py:269
  290.4 9.3 %collective-permute-start.48 = (bf16[96,768]{1,0:T(8,128)(2,1)S(1)}, bf16[96,768]{1,0:T(8,128)(2,1)S(1)}, u32[]{:S(2)}, u32[]{:S(2)}) collective-permute-start(bf16[96,768]{1,0:T(8,128)(2,1)S(1)} %fusion.44), channel_id=1, source_target_pairs={{0,2},{1,3},{2,0},{3,1},{4,6},{5,7},{6,4},{7,5},{8,10},{9,11},{10,... | collective-permute-start | bytes 442376 | tf_op jit(solution)/shard_map/ppermute | solution.py:284
  (81 other events, 446.2 us)
where the time goes:
time: 305 us; the launch traced here: 303 us
  waiting for transfers between devices  78.2 us (26%)
  local copies, waits for them, and re-layouts  53.2 us (17%)
  starting transfers between devices  48.3 us (16%)
  other arithmetic  46.8 us (15%)
  Pallas kernels  38.2 us (13%)
  matrix products  36.2 us (12%)
    ppermute x16, waiting for transfers between devices, tp_swap(): return lax.ppermute(value, 'tp', [(i, i ^ mask) for i in range(self.n_tp)])  40.4 us
    pallas_call x3, Pallas kernels, attention_call(): pl.pallas_call(kernel, grid_spec=pltpu.PrefetchScalarGridSpec(num_scalar_...  34.3 us
    ppermute x9, waiting for transfers between devices, half_swap(): return lax.ppermute(value, 'ctx', [(i, i ^ 2) for i in range(self.n_ctx)])  26.7 us
    ppermute x16, starting transfers between devices, tp_swap(): return lax.ppermute(value, 'tp', [(i, i ^ mask) for i in range(self.n_tp)])  20.1 us
    unnamed x168, local copies, waits for them, and re-layouts  17.7 us
    another operation x28, other arithmetic, ordered(): return jnp.stack([first, second], axis)  15.3 us
    dot_general x10, matrix products, dot_nt(): lax.dot_general(left, right, (((1,), (1,)), ((), ())), preferred_element_...  15.3 us
    ppermute x9, starting transfers between devices, half_swap(): return lax.ppermute(value, 'ctx', [(i, i ^ 2) for i in range(self.n_ctx)])  13.7 us
  transfers between devices with their start and end apart: 50, of which 15 were waited for; matrix products, arithmetic and copies ran while one was open for 35% of the time, Pallas kernels for 13%

commit v1 on v0

--- a/solution.py
+++ b/solution.py
@@ -64,28 +64,37 @@
         body(block, head, pl.ds(pl.multiple_of(block * local, local), local), pl.ds(head, 1))
 
 
+def head_rows(head):
+    return slice(head * HDIM, (head + 1) * HDIM)
+
+
 def prepare_kernel(
     meta, tokens_ref, cot_ref, gain_ref, stream_ref, unit_ref, inverse_ref, cot_out_ref, normed_ref,
     two_ref
 ):
     local, narrow = tokens_ref.shape
-    inside = lax.broadcasted_iota(jnp.int32, (local, narrow + 1), 1) < narrow
-    stream_ref[:, :narrow] = tokens_ref[...].astype(SINGLE)
-    part = jnp.where(inside, stream_ref[...], 0.0)
-    stream = jnp.where(inside, part, -jnp.sum(part, -1, keepdims=True))
-    inverse = lax.rsqrt(row_mean(stream * stream) + EPSILON)
-    unit = stream * inverse
-    normed = (unit * gain_ref[...]).astype(LOW)
-    stream_ref[...] = stream
-    unit_ref[...] = unit
-    inverse_ref[...] = inverse
-    normed_ref[...] = normed
-    two_ref[:, : narrow + 1] = normed
-    position = meta[3] * local + lax.broadcasted_iota(jnp.int32, (local, 1), 0)
-    cot_out_ref[:, :narrow] = cot_ref[...].astype(SINGLE)
-    cot = jnp.where(inside & (position < meta[2]), cot_out_ref[...], 0.0)
-    cot_out_ref[...] = cot
-    two_ref[:, narrow + 1 :] = (cot - row_mean(cot)).astype(LOW)
+    size = local // 4
+    inside = lax.broadcasted_iota(jnp.int32, (size, narrow + 1), 1) < narrow
+
+    @pl.loop(0, 4)
+    def _(at):
+        rows = pl.ds(pl.multiple_of(at * size, size), size)
+        stream_ref[rows, :narrow] = tokens_ref[rows, :].astype(SINGLE)
+        part = jnp.where(inside, stream_ref[rows, :], 0.0)
+        stream = jnp.where(inside, part, -jnp.sum(part, -1, keepdims=True))
+        inverse = lax.rsqrt(row_mean(stream * stream) + EPSILON)
+        unit = stream * inverse
+        normed = (unit * gain_ref[...]).astype(LOW)
+        stream_ref[rows, :] = stream
+        unit_ref[rows, :] = unit
+        inverse_ref[rows, :] = inverse
+        normed_ref[rows, :] = normed
+        two_ref[rows, : narrow + 1] = normed
+        position = lax.broadcasted_iota(jnp.int32, (size, 1), 0) + meta[3] * local + at * size
+        cot_out_ref[rows, :narrow] = cot_ref[rows, :].astype(SINGLE)
+        cot = jnp.where(inside & (position < meta[2]), cot_out_ref[rows, :], 0.0)
+        cot_out_ref[rows, :] = cot
+        two_ref[rows, narrow + 1 :] = (cot - row_mean(cot)).astype(LOW)
 
 
 def prepare(meta, tokens, cotangent, gain):
@@ -135,56 +144,60 @@
 def far_backward_kernel(
     meta, q_ref, k_ref, v_ref, grad_ref, out_ref, log_ref, dkv_ref, inner_ref, mix_ref, sums
 ):
-    width = dkv_ref.shape[1] // 2
-    local = q_ref.shape[0] // 2
+    rows_all, width = q_ref.shape[0], dkv_ref.shape[1] // 2
+    local = rows_all // 2
     scale = jnp.asarray(1.0 / math.sqrt(HDIM), LOW)
     sums[...] = jnp.zeros_like(sums)
-    mix_ref[...] = jnp.zeros_like(mix_ref)
-
-    def body(block, head, rows, line):
+
+    @pl.loop(0, 2)
+    def _(block):
         mask = far_mask(meta, local)
-        query = half_of(q_ref[rows, :], head) * scale
-        out_grad = half_of(grad_ref[rows, :], head)
-        inner = out_grad.astype(SINGLE) * out_ref[rows, :].astype(SINGLE)
-        inner = jnp.sum(inner.T, 0, keepdims=True)
-        inner_ref[0, line, rows] = inner
-        scores = jnp.where(mask, dot_nt(k_ref[...], query), MASKED)
-        probs = jnp.exp(scores - log_ref[0, line, rows])
-        grads = (probs * (dot_nt(v_ref[...], out_grad) - inner)).astype(LOW)
-        sums[0] += dot(grads, query)
-        sums[1] += dot(probs.astype(LOW), out_grad)
-        mix_ref[0, :, rows] += dot_tn(half_of(k_ref[...], head), grads)
-
-    each_head(local, body)
+        rows = pl.ds(pl.multiple_of(block * local, local), local)
+        product = (grad_ref[rows, :].astype(SINGLE) * out_ref[rows, :].astype(SINGLE)).T
+        for head in (0, 1):
+            query = half_of(q_ref[rows, :], head) * scale
+            out_grad = half_of(grad_ref[rows, :], head)
+            log_total = log_ref[0, head : head + 1, rows]
+            inner = jnp.sum(product[head_rows(head)], 0, keepdims=True)
+            inner_ref[0, head : head + 1, rows] = inner
+            probs = jnp.exp(jnp.where(mask, dot_nt(k_ref[...], query), MASKED) - log_total)
+            grads = (probs * (dot_nt(v_ref[...], out_grad) - inner)).astype(LOW)
+            sums[0] += dot(grads, query)
+            sums[1] += dot(probs.astype(LOW), out_grad)
+            mix_ref[0, head_rows(head), rows] = dot_tn(k_ref[...], grads)[head_rows(head)]
+
     lanes = pl.multiple_of(pl.program_id(0) * PAIR, PAIR)
     dkv_ref[:, pl.ds(lanes, PAIR)] = sums[0].astype(LOW)
     dkv_ref[:, pl.ds(width + lanes, PAIR)] = sums[1].astype(LOW)
 
 
 def near_backward_kernel(
-    meta, q_ref, k_ref, v_ref, grad_ref, log_ref, inner_ref, mix_ref, out_ref, sums, mix
+    meta, q_ref, k_ref, v_ref, grad_ref, log_ref, inner_ref, mix_ref, out_ref, sums
 ):
-    width = out_ref.shape[1] // 3
-    local = q_ref.shape[0] // 2
+    rows_all, width = q_ref.shape[0], out_ref.shape[1] // 3
+    lanes = pl.multiple_of(pl.program_id(0) * PAIR, PAIR)
+    local = rows_all // 2
     scale = 1.0 / math.sqrt(HDIM)
     sums[...] = jnp.zeros_like(sums)
-    mix[...] = mix_ref[0]
-
-    def body(block, head, rows, line):
+
+    @pl.loop(0, 2)
+    def _(block):
         mask = near_mask(meta, block, local)
-        query = half_of(q_ref[rows, :], head) * jnp.asarray(scale, LOW)
-        out_grad = half_of(grad_ref[rows, :], head)
-        scores = jnp.where(mask, dot_nt(k_ref[...], query), MASKED)
-        probs = jnp.exp(scores - log_ref[0, line, rows])
-        inner = inner_ref[0, line, rows]
-        grads = (probs * (dot_nt(v_ref[...], out_grad) - inner)).astype(LOW)
-        sums[0] += dot(grads, query)
-        sums[1] += dot(probs.astype(LOW), out_grad)
-        mix[:, rows] += dot_tn(half_of(k_ref[...], head), grads)
-
-    each_head(local, body)
-    lanes = pl.multiple_of(pl.program_id(0) * PAIR, PAIR)
-    out_ref[:, pl.ds(lanes, PAIR)] = (mix[...] * scale).T.astype(LOW)
+        rows = pl.ds(pl.multiple_of(block * local, local), local)
+        parts = []
+        for head in (0, 1):
+            query = half_of(q_ref[rows, :], head) * jnp.asarray(scale, LOW)
+            out_grad = half_of(grad_ref[rows, :], head)
+            log_total = log_ref[0, head : head + 1, rows]
+            inner = inner_ref[0, head : head + 1, rows]
+            probs = jnp.exp(jnp.where(mask, dot_nt(k_ref[...], query), MASKED) - log_total)
+            grads = (probs * (dot_nt(v_ref[...], out_grad) - inner)).astype(LOW)
+            sums[0] += dot(grads, query)
+            sums[1] += dot(probs.astype(LOW), out_grad)
+            mixed = dot_tn(k_ref[...], grads)[head_rows(head)]
+            parts.append((mix_ref[0, head_rows(head), rows] + mixed) * scale)
+        out_ref[rows, pl.ds(lanes, PAIR)] = jnp.concatenate(parts, 0).T.astype(LOW)
+
     out_ref[:, pl.ds(width + lanes, PAIR)] = sums[0].astype(LOW)
     out_ref[:, pl.ds(2 * width + lanes, PAIR)] = sums[1].astype(LOW)
 
@@ -245,7 +258,7 @@
         [(0, near), (1, near), (2, near), (0, grads), ("row", logs), ("row", inner),
          ("mix", mixed)],
         [("three", LOW)],
-        [pltpu.VMEM((2, rows, PAIR), SINGLE), pltpu.VMEM((PAIR, rows), SINGLE)],
+        [pltpu.VMEM((2, rows, PAIR), SINGLE)],
     )[0]
 
 
@@ -313,18 +326,33 @@
         rows, width = value.shape
         return value.reshape(self.n_shard, 2, rows // (2 * self.n_shard), width)
 
+    def step(self, values, index, axis, swap):
+        pick = lambda value, at: lax.dynamic_index_in_dim(value, at, axis, False)
+        sent = [pick(value, 1 - index).astype(LOW) for value in values]
+        sent = jnp.concatenate(sent, -1) if len(sent) > 1 else sent[0]
+        got, steps, start = swap(sent), [], 0
+        for value in values:
+            stop = start + value.shape[-1]
+            steps.append((pick(value, index), got[..., start:stop], sent))
+            start = stop
+        return steps
+
+    def half_steps(self, values, axis):
+        return self.step(values, self.half, axis, self.half_swap)
+
     def half_step(self, value, axis):
-        sent = lax.dynamic_index_in_dim(value, 1 - self.half, axis, False).astype(LOW)
-        kept = lax.dynamic_index_in_dim(value, self.half, axis, False)
-        return kept, self.half_swap(sent), sent
+        return self.half_steps([value], axis)[0]
+
+    def shard_steps(self, values):
+        if self.n_shard == 2:
+            return self.step(values, self.shard, 0, self.shard_swap)
+        kept = [
+            lax.psum_scatter(value, "shard", scatter_dimension=0, tiled=False) for value in values
+        ]
+        return [(value, jnp.zeros_like(value, LOW), value) for value in kept]
 
     def shard_step(self, value):
-        if self.n_shard == 2:
-            sent = lax.dynamic_index_in_dim(value, 1 - self.shard, 0, False).astype(LOW)
-            kept = lax.dynamic_index_in_dim(value, self.shard, 0, False)
-            return kept, self.shard_swap(sent), sent
-        kept = lax.psum_scatter(value, "shard", scatter_dimension=0, tiled=False)
-        return kept, jnp.zeros_like(kept, LOW), kept
+        return self.shard_steps([value])[0]
 
     def block_step(self, value):
         pieces = value.reshape(2, -1, value.shape[1])
@@ -397,9 +425,8 @@
     sequence = after(place.tp, other_a)
     length = lax.dynamic_index_in_dim(lengths, sequence, 0, False)
     meta = jnp.stack([place.half, place.core, length, place.ctx]).astype(jnp.int32)
-    tokens_low, cot_low = (
-        lax.dynamic_index_in_dim(item, sequence, 0, False) for item in (tokens, cotangent)
-    )
+    tokens_low = lax.dynamic_index_in_dim(tokens, sequence, 0, False)
+    cot_low = lax.dynamic_index_in_dim(cotangent, after(sequence, tokens_low), 0, False)
     stream, first_unit, first_inverse, cot_full, normed_own, own_two = prepare(
         meta, tokens_low, cot_low, first_gain.reshape(1, wide)
     )
@@ -512,30 +539,33 @@
     sum_h, sum_r = added(step_h, kv_weight_grad), added(step_r, kv_weight_grad)
     mlp_sent = jnp.concatenate([sum_h[:, units:], sum_r[:, units:]], 1).astype(LOW)
     mlp = (jnp.concatenate([sum_h[:, :units], sum_r[:, :units]], 1), place.tp_swap(mlp_sent, 1))
-    query_exit_grad = jnp.concatenate([query_weight_grad, exit_weight_grad], 1)
-    step_qe = place.shard_step(place.split_rows(query_exit_grad))
+    step_q, step_e = place.shard_steps(
+        [place.split_rows(query_weight_grad), place.split_rows(exit_weight_grad)]
+    )
     step_kv = place.half_step(place.split_rows(kv_weight_grad), 1)
     tokens_pair = place.ordered(
-        place.tp // 2, tokens_rows, after(tokens_far, step_kv[2], step_qe[2])
+        place.tp // 2, tokens_rows, after(tokens_far, step_kv[2], step_q[2])
     )
     tokens_near = place.tp_swap(tokens_pair, 1)
-    mlp = place.block_step(added(mlp, tokens_pair))
+    result = place.tp_all(result_pair, after(result_near, tokens_pair))[:, :, :narrow]
+    mlp = place.block_step(added(mlp, tokens_pair, result))
     mlp_first = mlp[2]
-    step_qe = place.half_step(added(step_qe, mlp_first), 0)
+    step_q, step_e = place.half_steps(
+        [added(step_q, mlp_first), added(step_e, mlp_first)], 0
+    )
     step_kv = place.shard_step(added(step_kv, mlp_first))
-    sums = jnp.concatenate([added(step_qe), added(step_kv)], 1)
+    sums, sum_kv = [added(step_q), added(step_e)], added(step_kv)
+    sums += [sum_kv[:, :width], sum_kv[:, width:]]
     sums = [
-        jnp.concatenate(
-            [sums[:, at * width + low : at * width + low + head_width] for at in range(4)], 1
-        )
+        jnp.concatenate([value[:, low : low + head_width] for value in sums], 1)
         for low in (0, head_width)
     ]
-    heads = added((sums[0], place.tp_swap(sums[1].astype(LOW), 1)), tokens_near)
+    heads = place.tp_swap(after(sums[1].astype(LOW), mlp[1]), 1)
+    heads = added((sums[0], heads), tokens_near)
     heads_sum = heads
     heads = place.block_step(heads)
-    result = place.tp_all(result_pair, after(result_near, tokens_pair))[:, :, :narrow]
+    tokens_grad = place.tp_all(tokens_pair, after(tokens_near, heads[2]))[:, :, :narrow]
     mlp, heads = added(mlp, heads[0]), added(heads)
-    tokens_grad = place.tp_all(tokens_pair, tokens_near)[:, :, :narrow]
     at = lambda index: heads[:, index * head_width : (index + 1) * head_width]
     entry_grad = jnp.stack([at(0), at(2), at(3)])
     exit_grad = at(1).T

time: 305 us -> 291 us (0.954)
  local copies, waits for them, and re-layouts: 53.2 us -> 44.9 us
  waiting for transfers between devices: 78.2 us -> 83.9 us
  matrix products: 36.2 us -> 31.8 us
  starting transfers between devices: 48.3 us -> 44.6 us
  Pallas kernels: 38.2 us -> 34.9 us
    ppermute x9, waiting for transfers between devices: 26.7 us -> 32.2 us  [half_swap(): return lax.ppermute(value, 'ctx', [(i, i ^ 2) for i in range(self.n_ctx)])]
    dot_general x6, matrix products: 9.81 us -> 5.65 us  [dot_tn(): lax.dot_general(left, right, (((0,), (0,)), ((), ())), preferred_element_...]
    pallas_call x3, Pallas kernels: 34.3 us -> 30.6 us  [attention_call(): pl.pallas_call(kernel, grid_spec=pltpu.PrefetchScalarGridSpec(num_scalar_...]
    add x10 -> x13, other arithmetic: 11.1 us -> 12.5 us  [added(): return kept + after(arriving, *gates).astype(SINGLE)]
    convert_element_type x8 -> x10, local copies, waits for them, and re-layouts: 7.52 us -> 6.16 us  [step(): sent = [pick(value, 1 - index).astype(LOW) for value in values]]
    unnamed x168 -> x190, local copies, waits for them, and re-layouts: 17.7 us -> 19 us
    dynamic_slice x3 -> x4, local copies, waits for them, and re-layouts: 7.13 us -> 6.72 us  [the longest x2 4.08 us: shards(): lax.dynamic_index_in_dim(cotangent, after(sequence, tokens_low), 0, False)]
  transfers between devices with their start and end apart: 50 -> 50, of which waited for: 15 -> 17; matrix products, arithmetic and copies ran while one was open for 35% -> 29% of each run, Pallas kernels for 13% -> 12%
where the time goes in v1:
time: 291 us; the launch traced here: 289 us
  waiting for transfers between devices  83.9 us (29%)
  other arithmetic  46.4 us (16%)
  local copies, waits for them, and re-layouts  44.9 us (15%)
  starting transfers between devices  44.6 us (15%)
  Pallas kernels  34.9 us (12%)
  matrix products  31.8 us (11%)
    ppermute x16, waiting for transfers between devices, tp_swap(): return lax.ppermute(value, 'tp', [(i, i ^ mask) for i in range(self.n_tp)])  43.4 us
    ppermute x9, waiting for transfers between devices, half_swap(): return lax.ppermute(value, 'ctx', [(i, i ^ 2) for i in range(self.n_ctx)])  32.2 us
    pallas_call x3, Pallas kernels, attention_call(): pl.pallas_call(kernel, grid_spec=pltpu.PrefetchScalarGridSpec(num_scalar_...  30.6 us
    unnamed x190, local copies, waits for them, and re-layouts  19 us
    ppermute x16, starting transfers between devices, tp_swap(): return lax.ppermute(value, 'tp', [(i, i ^ mask) for i in range(self.n_tp)])  17.5 us
    dot_general x10, matrix products, dot_nt(): lax.dot_general(left, right, (((1,), (1,)), ((), ())), preferred_element_...  15 us
    another operation x28, other arithmetic, ordered(): return jnp.stack([first, second], axis)  14.7 us
    add x13, other arithmetic, added(): return kept + after(arriving, *gates).astype(SINGLE)  12.5 us
  transfers between devices with their start and end apart: 50, of which 17 were waited for; matrix products, arithmetic and copies ran while one was open for 29% of the time, Pallas kernels for 12%

profile of v1, /device:TPU:0, one launch (start us, length us, event | category | flops | bytes accessed | tf_op | source)
XLA Modules:
  0.0 289.2 jit_solution(7166259768674364582)
XLA Ops:
  2.3 4.1 %collective-permute-start.8 = (f32[1152]{0:T(1024)S(1)}, f32[1152]{0:T(1024)S(1)}, u32[]{:S(2)}, u32[]{:S(2)}) collective-permute-start(f32[1152]{0:T(1024)S(1)} %constant_dynamic-update-slice_fusion.13), channel_id=1, source_target_pairs={{0,2},{1,3},{2,0},{3,1},{4,6},{5,7},{6,4},{7,5},{8,10},{9,11},{10,... | collective-permute-start | bytes 13832 | tf_op jit(solution)/shard_map/ppermute | solution.py:297
  8.3 1.9 collective-permute-start.9
  10.2 7.4 %collective-permute-done = bf16[96,768]{1,0:T(8,128)(2,1)S(1)} collective-permute-done((bf16[96,768]{1,0:T(8,128)(2,1)S(1)}, bf16[96,768]{1,0:T(8,128)(2,1)S(1)}, u32[]{:S(2)}, u32[]{:S(2)}) %collective-permute-start) | collective-permute-done | bytes 147488 | tf_op jit(solution)/shard_map/ppermute | solution.py:297
  21.3 8.6 %collective-permute-done.2 = bf16[192,768]{1,0:T(8,128)(2,1)S(1)} collective-permute-done((bf16[192,768]{1,0:T(8,128)(2,1)S(1)}, bf16[192,768]{1,0:T(8,128)(2,1)S(1)}, u32[]{:S(2)}, u32[]{:S(2)}) %collective-permute-start.2) | collective-permute-done | bytes 294944 | tf_op jit(solution)/shard_map/ppermute | solution.py:297
  30.8 1.8 copy.33
  35.9 1.6 collective-permute-start.6
  37.5 2.2 constant_dynamic-slice_fusion.1
  39.7 1.9 copy.34
  42.9 4.3 %prepare.1 = (f32[256,768]{1,0:T(8,128)}, f32[256,768]{1,0:T(8,128)}, f32[256,1]{1,0:T(8,128)}, f32[256,768]{1,0:T(8,128)}, bf16[256,768]{1,0:T(8,128)(2,1)}, /*index=5*/bf16[256,1536]{1,0:T(8,128)(2,1)}) custom-call(s32[4]{0:T(128)} %pad_add_fusion.meta, bf16[256,767]{1,0:T(8,128)(2,1)} %bitcast.213, bf16[256,767]{1,0:T(8,128)(2,1)} %bitcast.214, ...), custom_call_target="tpu_custom_call" | custom-call | flops 3932160 | bytes 3932160 | tf_op jit(solution)/shard_map/prepare/pallas_call | solution.py:105
  47.2 2.6 collective-permute-start.10
  52.9 1.8 collective-permute-start.14
  54.7 15.3 %collective-permute-done.5 = bf16[2,192,768]{2,1,0:T(8,128)(2,1)S(1)} collective-permute-done((bf16[2,192,768]{2,1,0:T(8,128)(2,1)S(1)}, bf16[2,192,768]{2,1,0:T(8,128)(2,1)S(1)}, u32[]{:S(2)}, u32[]{:S(2)}) %collective-permute-start.5) | collective-permute-done | bytes 589856 | tf_op jit(solution)/shard_map/ppermute | solution.py:285
  70.7 2.5 collective-permute-start.15
  74.0 2.2 fusion.7.q_ref.k_ref.v_ref
  76.7 8.2 %collective-permute-done.15 = bf16[192,1536]{1,0:T(8,128)(2,1)S(1)} collective-permute-done((bf16[192,1536]{1,0:T(8,128)(2,1)S(1)}, bf16[192,1536]{1,0:T(8,128)(2,1)S(1)}, u32[]{:S(2)}, u32[]{:S(2)}) %collective-permute-start.15) | collective-permute-done | bytes 589856 | tf_op jit(solution)/shard_map/ppermute | solution.py:285
  86.8 5.7 %collective-permute-done.16 = bf16[192,1536]{1,0:T(8,128)(2,1)S(1)} collective-permute-done((bf16[192,1536]{1,0:T(8,128)(2,1)S(1)}, bf16[192,1536]{1,0:T(8,128)(2,1)S(1)}, u32[]{:S(2)}, u32[]{:S(2)}) %collective-permute-start.16) | collective-permute-done | bytes 589856 | tf_op jit(solution)/shard_map/ppermute | solution.py:294
  96.3 1.7 add_convert_fusion.kf_ref.vf_ref.k_ref.v_ref
  98.0 13.2 %attend.1 = (bf16[512,384]{1,0:T(8,128)(2,1)}, f32[3,2,512]{2,1,0:T(2,128)}) custom-call(s32[4]{0:T(128)} %pad_add_fusion.meta, bf16[512,1152]{1,0:T(8,128)(2,1)} %fusion.7.q_ref.k_ref.v_ref, bf16[512,1152]{1,0:T(8,128)(2,1)} %fusion.7.q_ref.k_ref.v_ref, bf16[512,1152]{1,0:T(8,128)(2,1)} %fusion.7.q_ref.k_ref.v_ref, ...), custom_call_target="tpu_custom_call" | custom-call | flops 805306368 | bytes 3145728 | tf_op jit(solution)/shard_map/attend/pallas_call | solution.py:217
  111.2 2.4 convolution_convert_fusion.5
  116.9 3.3 %collective-permute-done.19 = bf16[2,192,1536]{2,1,0:T(8,128)(2,1)} collective-permute-done((bf16[2,192,1536]{2,1,0:T(8,128)(2,1)}, bf16[2,192,1536]{2,1,0:T(8,128)(2,1)}, u32[]{:S(2)}, u32[]{:S(2)}) %collective-permute-start.19) | collective-permute-done | bytes 1179680 | tf_op jit(solution)/shard_map/ppermute | solution.py:285
  123.4 1.6 select_bitcast_fusion.3
  128.1 2.0 multiply_convert_fusion
  132.7 3.9 %convert_reduce_fusion = (f32[1536]{0:T(1024)S(1)}, bf16[512,1536]{1,0:T(8,128)(2,1)}) fusion(f32[512,1536]{1,0:T(8,128)S(1)} %get-tuple-element.238, bf16[768,1536]{1,0:T(8,128)(2,1)S(1)} %bitcast.208, bf16[512,1536]{1,0:T(8,128)(2,1)S(1)} %copy-done.23), kind=kOutput, calls=%fused_computation.11 | convolution fusion | flops 1225259520 | bytes 7870464 | tf_op jit(solution)/shard_map/dot_general | solution.py:24
  136.6 2.9 convolution_convert_fusion.3
  145.1 2.5 collective-permute-start.22
  157.6 8.1 %attend_far_back.1 = (bf16[512,768]{1,0:T(8,128)(2,1)}, f32[3,2,512]{2,1,0:T(2,128)}, f32[3,128,512]{2,1,0:T(8,128)}) custom-call(s32[4]{0:T(128)} %pad_add_fusion.meta, bf16[512,1152]{1,0:T(8,128)(2,1)} %fusion.7.q_ref.k_ref.v_ref, bf16[512,768]{1,0:T(8,128)(2,1)} %add_convert_fusion.kf_ref.vf_ref.k_ref.v_ref, ...), custom_call_target="tpu_custom_call" | custom-call | flops 805306368 | bytes 3145728 | tf_op jit(solution)/shard_map/attend_far_back/pallas_call | solution.py:217
  165.8 1.6 convolution_convert_fusion.1
  169.2 1.6 select_bitcast_fusion.19
  176.0 9.2 %attend_near_back.1 = bf16[512,1152]{1,0:T(8,128)(2,1)} custom-call(s32[4]{0:T(128)} %pad_add_fusion.meta, bf16[512,1152]{1,0:T(8,128)(2,1)} %fusion.7.q_ref.k_ref.v_ref, bf16[512,1152]{1,0:T(8,128)(2,1)} %fusion.7.q_ref.k_ref.v_ref, bf16[512,1152]{1,0:T(8,128)(2,1)} %fusion.7.q_ref.k_ref.v_ref, bf16[512,384]{1,0:T(8,128)(2,1)} %convolution_convert_fusion.2.grad_ref, ...), custom_call_target="tpu_custom_call" | custom-call | flops 805306368 | bytes 3145728 | tf_op jit(solution)/shard_map/attend_near_back/pallas_call | solution.py:217
  185.3 1.9 convolution_convert_fusion
  187.2 1.8 fusion.30
  189.0 2.3 bitcast_add_fusion
  192.4 3.4 %collective-permute-start.35 = (bf16[192,1536]{1,0:T(8,128)(2,1)}, bf16[192,1536]{1,0:T(8,128)(2,1)}, u32[]{:S(2)}, u32[]{:S(2)}) collective-permute-start(bf16[192,1536]{1,0:T(8,128)(2,1)} %fusion.27), channel_id=1, source_target_pairs={{0,8},{4,12},{8,0},{12,4},{1,9},{5,13},{9,1},{13,5},{2,10},{6,14},... | collective-permute-start | bytes 1769480 | tf_op jit(solution)/shard_map/ppermute | solution.py:285
  195.8 1.6 bitcast_add_fusion.1
  199.9 1.9 multiply_reduce_fusion.1
  213.7 1.6 bitcast_add_fusion.3
  215.3 2.0 bitcast_add_fusion.4
  219.7 5.5 %collective-permute-done.31 = bf16[256,768]{1,0:T(8,128)(2,1)} collective-permute-done((bf16[256,768]{1,0:T(8,128)(2,1)}, bf16[256,768]{1,0:T(8,128)(2,1)}, u32[]{:S(2)}, u32[]{:S(2)}) %collective-permute-start.31) | collective-permute-done | bytes 393248 | tf_op jit(solution)/shard_map/ppermute | solution.py:297
  230.9 6.9 %collective-permute-done.36 = bf16[192,1536]{1,0:T(8,128)(2,1)S(1)} collective-permute-done((bf16[192,1536]{1,0:T(8,128)(2,1)S(1)}, bf16[192,1536]{1,0:T(8,128)(2,1)S(1)}, u32[]{:S(2)}, u32[]{:S(2)}) %collective-permute-start.36) | collective-permute-done | bytes 589856 | tf_op jit(solution)/shard_map/ppermute | solution.py:297
  238.1 1.6 fusion.68
  245.1 5.3 %collective-permute-done.38 = bf16[192,768]{1,0:T(8,128)(2,1)S(1)} collective-permute-done((bf16[192,768]{1,0:T(8,128)(2,1)S(1)}, bf16[192,768]{1,0:T(8,128)(2,1)S(1)}, u32[]{:S(2)}, u32[]{:S(2)}) %collective-permute-start.38) | collective-permute-done | bytes 294944 | tf_op jit(solution)/shard_map/ppermute | solution.py:285
  253.8 1.8 collective-permute-done.41
  255.6 3.0 %collective-permute-start.42 = (bf16[192,768]{1,0:T(8,128)(2,1)}, bf16[192,768]{1,0:T(8,128)(2,1)}, u32[]{:S(2)}, u32[]{:S(2)}) collective-permute-start(bf16[192,768]{1,0:T(8,128)(2,1)} %pad_maximum_fusion.28), channel_id=1, source_target_pairs={{0,1},{1,0},{2,3},{3,2},{4,5},{5,4},{6,7},{7,6},{8,9},{9,8},{10,11... | collective-permute-start | bytes 884744 | tf_op jit(solution)/shard_map/ppermute | solution.py:297
  259.6 2.2 copy.40
  262.7 4.7 %collective-permute-done.42 = bf16[192,768]{1,0:T(8,128)(2,1)} collective-permute-done((bf16[192,768]{1,0:T(8,128)(2,1)}, bf16[192,768]{1,0:T(8,128)(2,1)}, u32[]{:S(2)}, u32[]{:S(2)}) %collective-permute-start.42) | collective-permute-done | bytes 294944 | tf_op jit(solution)/shard_map/ppermute | solution.py:297
  269.1 4.4 %collective-permute-done.48 = f32[7680]{0:T(1024)S(1)} collective-permute-done((f32[7680]{0:T(1024)S(1)}, f32[7680]{0:T(1024)S(1)}, u32[]{:S(2)}, u32[]{:S(2)}) %collective-permute-start.48) | collective-permute-done | bytes 30752 | tf_op jit(solution)/shard_map/ppermute | solution.py:297
  278.1 2.2 copy.41
  280.3 4.1 %collective-permute-done.49 = bf16[96,768]{1,0:T(8,128)(2,1)} collective-permute-done((bf16[96,768]{1,0:T(8,128)(2,1)}, bf16[96,768]{1,0:T(8,128)(2,1)}, u32[]{:S(2)}, u32[]{:S(2)}) %collective-permute-start.49) | collective-permute-done | bytes 147488 | tf_op jit(solution)/shard_map/ppermute | solution.py:297
  (429 shorter events, 102.2 us)
Async XLA Ops:
  2.3 6.0 %collective-permute-start.8 = (f32[1152]{0:T(1024)S(1)}, f32[1152]{0:T(1024)S(1)}, u32[]{:S(2)}, u32[]{:S(2)}) collective-permute-start(f32[1152]{0:T(1024)S(1)} %constant_dynamic-update-slice_fusion.13), channel_id=1, source_target_pairs={{0,2},{1,3},{2,0},{3,1},{4,6},{5,7},{6,4},{7,5},{8,10},{9,11},{10,... | collective-permute-start | bytes 13832 | tf_op jit(solution)/shard_map/ppermute | solution.py:297
  8.2 9.4 %collective-permute-start = (bf16[96,768]{1,0:T(8,128)(2,1)S(1)}, bf16[96,768]{1,0:T(8,128)(2,1)S(1)}, u32[]{:S(2)}, u32[]{:S(2)}) collective-permute-start(bf16[96,768]{1,0:T(8,128)(2,1)S(1)} %pad_maximum_fusion.30), channel_id=1, source_target_pairs={{0,2},{1,3},{2,0},{3,1},{4,6},{5,7},{6,4},{7,5},{8,10},{9,11},{10,... | collective-permute-start | bytes 442376 | tf_op jit(solution)/shard_map/ppermute | solution.py:297
  8.3 11.1 %collective-permute-start.9 = (f32[1152]{0:T(1024)S(1)}, f32[1152]{0:T(1024)S(1)}, u32[]{:S(2)}, u32[]{:S(2)}) collective-permute-start(f32[1152]{0:T(1024)S(1)} %broadcast_select_fusion.12), channel_id=1, source_target_pairs={{0,1},{1,0},{2,3},{3,2},{4,5},{5,4},{6,7},{7,6},{8,9},{9,8},{10,11... | collective-permute-start | bytes 13832 | tf_op jit(solution)/shard_map/ppermute | solution.py:297
  17.7 2.6 collective-permute-start.1
  20.5 9.5 %collective-permute-start.2 = (bf16[192,768]{1,0:T(8,128)(2,1)S(1)}, bf16[192,768]{1,0:T(8,128)(2,1)S(1)}, u32[]{:S(2)}, u32[]{:S(2)}) collective-permute-start(bf16[192,768]{1,0:T(8,128)(2,1)S(1)} %bitcast.211), channel_id=1, source_target_pairs={{0,1},{1,0},{2,3},{3,2},{4,5},{5,4},{6,7},{7,6},{8,9},{9,8},{10,11... | collective-permute-start | bytes 884744 | tf_op jit(solution)/shard_map/ppermute | solution.py:297
  33.2 16.7 %collective-permute-start.12 = (bf16[96,1536]{1,0:T(8,128)(2,1)S(1)}, bf16[96,1536]{1,0:T(8,128)(2,1)S(1)}, u32[]{:S(2)}, u32[]{:S(2)}) collective-permute-start(bf16[96,1536]{1,0:T(8,128)(2,1)S(1)} %pad_maximum_fusion.26), channel_id=1, source_target_pairs={{0,2},{1,3},{2,0},{3,1},{4,6},{5,7},{6,4},{7,5},{8,10},{9,11},{10,... | collective-permute-start | bytes 884744 | tf_op jit(solution)/shard_map/ppermute | solution.py:297
  34.3 16.2 %collective-permute-start.4 = (bf16[192,768]{1,0:T(8,128)(2,1)}, bf16[192,768]{1,0:T(8,128)(2,1)S(1)}, u32[]{:S(2)}, u32[]{:S(2)}) collective-permute-start(bf16[192,768]{1,0:T(8,128)(2,1)} %pad_maximum_fusion.24), channel_id=1, source_target_pairs={{0,16},{16,0},{1,17},{17,1},{2,18},{18,2},{3,19},{19,3},{4,20},{20... | collective-permute-start | bytes 884744 | tf_op jit(solution)/shard_map/ppermute | solution.py:294
  35.9 15.0 %collective-permute-start.6 = (bf16[192,768]{1,0:T(8,128)(2,1)S(1)}, bf16[192,768]{1,0:T(8,128)(2,1)S(1)}, u32[]{:S(2)}, u32[]{:S(2)}) collective-permute-start(bf16[192,768]{1,0:T(8,128)(2,1)S(1)} %pad_maximum_fusion.25), channel_id=1, source_target_pairs={{0,8},{4,12},{8,0},{12,4},{1,9},{5,13},{9,1},{13,5},{2,10},{6,14},... | collective-permute-start | bytes 884744 | tf_op jit(solution)/shard_map/ppermute | solution.py:285
  47.2 26.3 %collective-permute-start.10 = (bf16[256,768]{1,0:T(8,128)(2,1)}, bf16[256,768]{1,0:T(8,128)(2,1)S(1)}, u32[]{:S(2)}, u32[]{:S(2)}) collective-permute-start(bf16[256,768]{1,0:T(8,128)(2,1)} %get-tuple-element.74), channel_id=1, source_target_pairs={{0,8},{4,12},{1,9},{5,13},{2,10},{6,14},{3,11},{7,15},{16,24},{20,... | collective-permute-start | bytes 1179656 | tf_op jit(solution)/shard_map/ppermute | solution.py:288
  49.8 23.6 %collective-permute-start.3 = (bf16[256,1536]{1,0:T(8,128)(2,1)}, bf16[256,1536]{1,0:T(8,128)(2,1)S(1)}, u32[]{:S(2)}, u32[]{:S(2)}) collective-permute-start(bf16[256,1536]{1,0:T(8,128)(2,1)} %get-tuple-element.73), channel_id=1, source_target_pairs={{0,4},{4,0},{8,12},{12,8},{1,5},{5,1},{9,13},{13,9},{2,6},{6,2},{1... | collective-permute-start | bytes 2359304 | tf_op jit(solution)/shard_map/ppermute | solution.py:282
  49.9 2.9 collective-permute-start.13
  50.7 19.3 %collective-permute-start.5 = (bf16[2,192,768]{2,1,0:T(8,128)(2,1)S(1)}, bf16[2,192,768]{2,1,0:T(8,128)(2,1)S(1)}, u32[]{:S(2)}, u32[]{:S(2)}) collective-permute-start(bf16[2,192,768]{2,1,0:T(8,128)(2,1)S(1)} %pad_maximum_fusion.13), channel_id=1, source_target_pairs={{0,8},{4,12},{8,0},{12,4},{1,9},{5,13},{9,1},{13,5},{2,10},{6,14},... | collective-permute-start | bytes 1769480 | tf_op jit(solution)/shard_map/ppermute | solution.py:285
  51.2 19.0 %collective-permute-start.7 = (bf16[2,192,768]{2,1,0:T(8,128)(2,1)S(1)}, bf16[2,192,768]{2,1,0:T(8,128)(2,1)S(1)}, u32[]{:S(2)}, u32[]{:S(2)}) collective-permute-start(bf16[2,192,768]{2,1,0:T(8,128)(2,1)S(1)} %pad_maximum_fusion.14), channel_id=1, source_target_pairs={{0,16},{16,0},{1,17},{17,1},{2,18},{18,2},{3,19},{19,3},{4,20},{20... | collective-permute-start | bytes 1769480 | tf_op jit(solution)/shard_map/ppermute | solution.py:294
  52.9 17.7 %collective-permute-start.14 = (bf16[192,1536]{1,0:T(8,128)(2,1)S(1)}, bf16[192,1536]{1,0:T(8,128)(2,1)S(1)}, u32[]{:S(2)}, u32[]{:S(2)}) collective-permute-start(bf16[192,1536]{1,0:T(8,128)(2,1)S(1)} %bitcast.209), channel_id=1, source_target_pairs={{0,1},{1,0},{2,3},{3,2},{4,5},{5,4},{6,7},{7,6},{8,9},{9,8},{10,11... | collective-permute-start | bytes 1769480 | tf_op jit(solution)/shard_map/ppermute | solution.py:297
  70.7 14.3 %collective-permute-start.15 = (bf16[192,1536]{1,0:T(8,128)(2,1)S(1)}, bf16[192,1536]{1,0:T(8,128)(2,1)S(1)}, u32[]{:S(2)}, u32[]{:S(2)}) collective-permute-start(bf16[192,1536]{1,0:T(8,128)(2,1)S(1)} %get-tuple-element.77), channel_id=1, source_target_pairs={{0,8},{4,12},{8,0},{12,4},{1,9},{5,13},{9,1},{13,5},{2,10},{6,14},... | collective-permute-start | bytes 1769480 | tf_op jit(solution)/shard_map/ppermute | solution.py:285
  73.5 21.8 %collective-permute-start.11 = (bf16[256,768]{1,0:T(8,128)(2,1)S(1)}, bf16[256,768]{1,0:T(8,128)(2,1)S(1)}, u32[]{:S(2)}, u32[]{:S(2)}) collective-permute-start(bf16[256,768]{1,0:T(8,128)(2,1)S(1)} %collective-permute-done.10), channel_id=1, source_target_pairs={{0,4},{4,0},{8,12},{12,8},{1,5},{5,1},{9,13},{13,9},{2,6},{6,2},{1... | collective-permute-start | bytes 1179656 | tf_op jit(solution)/shard_map/ppermute | solution.py:282
  76.2 16.2 %collective-permute-start.16 = (bf16[192,1536]{1,0:T(8,128)(2,1)S(1)}, bf16[192,1536]{1,0:T(8,128)(2,1)S(1)}, u32[]{:S(2)}, u32[]{:S(2)}) collective-permute-start(bf16[192,1536]{1,0:T(8,128)(2,1)S(1)} %get-tuple-element.78), channel_id=1, source_target_pairs={{0,16},{16,0},{1,17},{17,1},{2,18},{18,2},{3,19},{19,3},{4,20},{20... | collective-permute-start | bytes 1769480 | tf_op jit(solution)/shard_map/ppermute | solution.py:294
  86.3 30.7 %collective-permute-start.18 = (bf16[2,192,1536]{2,1,0:T(8,128)(2,1)}, bf16[2,192,1536]{2,1,0:T(8,128)(2,1)}, u32[]{:S(2)}, u32[]{:S(2)}) collective-permute-start(bf16[2,192,1536]{2,1,0:T(8,128)(2,1)} %pad_maximum_fusion.7), channel_id=1, source_target_pairs={{0,16},{16,0},{1,17},{17,1},{2,18},{18,2},{3,19},{19,3},{4,20},{20... | collective-permute-start | bytes 3538952 | tf_op jit(solution)/shard_map/ppermute | solution.py:294
  93.8 26.5 %collective-permute-start.19 = (bf16[2,192,1536]{2,1,0:T(8,128)(2,1)}, bf16[2,192,1536]{2,1,0:T(8,128)(2,1)}, u32[]{:S(2)}, u32[]{:S(2)}) collective-permute-start(bf16[2,192,1536]{2,1,0:T(8,128)(2,1)} %pad_maximum_fusion.8), channel_id=1, source_target_pairs={{0,8},{4,12},{8,0},{12,4},{1,9},{5,13},{9,1},{13,5},{2,10},{6,14},... | collective-permute-start | bytes 3538952 | tf_op jit(solution)/shard_map/ppermute | solution.py:285
  113.6 2.1 collective-permute-start.17
  123.3 3.6 %collective-permute-start.20 = (bf16[256,768]{1,0:T(8,128)(2,1)S(1)}, bf16[256,768]{1,0:T(8,128)(2,1)S(1)}, u32[]{:S(2)}, u32[]{:S(2)}) collective-permute-start(bf16[256,768]{1,0:T(8,128)(2,1)S(1)} %multiply_convert_fusion.1), channel_id=1, source_target_pairs={{0,4},{4,0},{8,12},{12,8},{1,5},{5,1},{9,13},{13,9},{2,6},{6,2},{1... | collective-permute-start | bytes 1179656 | tf_op jit(solution)/shard_map/ppermute | solution.py:282
  139.5 3.5 %collective-permute-start.23 = (bf16[256,768]{1,0:T(8,128)(2,1)S(1)}, bf16[256,768]{1,0:T(8,128)(2,1)S(1)}, u32[]{:S(2)}, u32[]{:S(2)}) collective-permute-start(bf16[256,768]{1,0:T(8,128)(2,1)S(1)} %convolution_convert_fusion.3), channel_id=1, source_target_pairs={{0,4},{4,0},{8,12},{12,8},{1,5},{5,1},{9,13},{13,9},{2,6},{6,2},{1... | collective-permute-start | bytes 1179656 | tf_op jit(solution)/shard_map/ppermute | solution.py:282
  144.7 11.5 %collective-permute-start.24 = (bf16[256,768]{1,0:T(8,128)(2,1)S(1)}, bf16[256,768]{1,0:T(8,128)(2,1)S(1)}, u32[]{:S(2)}, u32[]{:S(2)}) collective-permute-start(bf16[256,768]{1,0:T(8,128)(2,1)S(1)} %get-tuple-element.165), channel_id=1, source_target_pairs={{0,4},{4,0},{8,12},{12,8},{1,5},{5,1},{9,13},{13,9},{2,6},{6,2},{1... | collective-permute-start | bytes 1179656 | tf_op jit(solution)/shard_map/ppermute | solution.py:282
  145.1 24.1 %collective-permute-start.22 = (bf16[256,768]{1,0:T(8,128)(2,1)}, bf16[256,768]{1,0:T(8,128)(2,1)}, u32[]{:S(2)}, u32[]{:S(2)}) collective-permute-start(bf16[256,768]{1,0:T(8,128)(2,1)} %subtract_convert_fusion.2), channel_id=1, source_target_pairs={{0,2},{1,3},{2,0},{3,1},{4,6},{5,7},{6,4},{7,5},{8,10},{9,11},{10,... | collective-permute-start | bytes 1179656 | tf_op jit(solution)/shard_map/ppermute | solution.py:297
  151.6 37.4 %collective-permute-start.30 = (bf16[2,192,1536]{2,1,0:T(8,128)(2,1)}, bf16[2,192,1536]{2,1,0:T(8,128)(2,1)}, u32[]{:S(2)}, u32[]{:S(2)}) collective-permute-start(bf16[2,192,1536]{2,1,0:T(8,128)(2,1)} %fusion.9), channel_id=1, source_target_pairs={{0,16},{16,0},{1,17},{17,1},{2,18},{18,2},{3,19},{19,3},{4,20},{20... | collective-permute-start | bytes 3538952 | tf_op jit(solution)/shard_map/ppermute | solution.py:294
  154.8 41.0 %collective-permute-start.29 = (bf16[2,192,1536]{2,1,0:T(8,128)(2,1)}, bf16[2,192,1536]{2,1,0:T(8,128)(2,1)}, u32[]{:S(2)}, u32[]{:S(2)}) collective-permute-start(bf16[2,192,1536]{2,1,0:T(8,128)(2,1)} %fusion.8), channel_id=1, source_target_pairs={{0,8},{4,12},{8,0},{12,4},{1,9},{5,13},{9,1},{13,5},{2,10},{6,14},... | collective-permute-start | bytes 3538952 | tf_op jit(solution)/shard_map/ppermute | solution.py:285
  167.9 6.0 %collective-permute-start.26 = (bf16[256,768]{1,0:T(8,128)(2,1)S(1)}, bf16[256,768]{1,0:T(8,128)(2,1)S(1)}, u32[]{:S(2)}, u32[]{:S(2)}) collective-permute-start(bf16[256,768]{1,0:T(8,128)(2,1)S(1)} %convolution_convert_fusion.1), channel_id=1, source_target_pairs={{0,4},{4,0},{8,12},{12,8},{1,5},{5,1},{9,13},{13,9},{2,6},{6,2},{1... | collective-permute-start | bytes 1179656 | tf_op jit(solution)/shard_map/ppermute | solution.py:282
  171.9 23.9 %collective-permute-start.25 = (bf16[2,256,768]{2,1,0:T(8,128)(2,1)}, bf16[2,256,768]{2,1,0:T(8,128)(2,1)}, u32[]{:S(2)}, u32[]{:S(2)}) collective-permute-start(bf16[2,256,768]{2,1,0:T(8,128)(2,1)} %pad_maximum_fusion.11), channel_id=1, source_target_pairs={{0,1},{1,0},{2,3},{3,2},{4,5},{5,4},{6,7},{7,6},{8,9},{9,8},{10,11... | collective-permute-start | bytes 2359304 | tf_op jit(solution)/shard_map/ppermute | solution.py:297
  174.7 21.0 %collective-permute-start.27 = (bf16[256,768]{1,0:T(8,128)(2,1)}, bf16[256,768]{1,0:T(8,128)(2,1)}, u32[]{:S(2)}, u32[]{:S(2)}) collective-permute-start(bf16[256,768]{1,0:T(8,128)(2,1)} %add_convert_fusion.1), channel_id=1, source_target_pairs={{8,0},{12,4},{9,1},{13,5},{10,2},{14,6},{11,3},{15,7},{24,16},{28,... | collective-permute-start | bytes 1179656 | tf_op jit(solution)/shard_map/ppermute | solution.py:291
  192.4 21.4 %collective-permute-start.35 = (bf16[192,1536]{1,0:T(8,128)(2,1)}, bf16[192,1536]{1,0:T(8,128)(2,1)}, u32[]{:S(2)}, u32[]{:S(2)}) collective-permute-start(bf16[192,1536]{1,0:T(8,128)(2,1)} %fusion.27), channel_id=1, source_target_pairs={{0,8},{4,12},{8,0},{12,4},{1,9},{5,13},{9,1},{13,5},{2,10},{6,14},... | collective-permute-start | bytes 1769480 | tf_op jit(solution)/shard_map/ppermute | solution.py:285
  195.7 4.2 %collective-permute-start.28 = (bf16[256,768]{1,0:T(8,128)(2,1)S(1)}, bf16[256,768]{1,0:T(8,128)(2,1)S(1)}, u32[]{:S(2)}, u32[]{:S(2)}) collective-permute-start(bf16[256,768]{1,0:T(8,128)(2,1)S(1)} %convolution_convert_fusion), channel_id=1, source_target_pairs={{0,4},{4,0},{8,12},{12,8},{1,5},{5,1},{9,13},{13,9},{2,6},{6,2},{1... | collective-permute-start | bytes 1179656 | tf_op jit(solution)/shard_map/ppermute | solution.py:282
  198.4 16.9 %collective-permute-start.34 = (bf16[192,1536]{1,0:T(8,128)(2,1)}, bf16[192,1536]{1,0:T(8,128)(2,1)}, u32[]{:S(2)}, u32[]{:S(2)}) collective-permute-start(bf16[192,1536]{1,0:T(8,128)(2,1)} %fusion.26), channel_id=1, source_target_pairs={{0,16},{16,0},{1,17},{17,1},{2,18},{18,2},{3,19},{19,3},{4,20},{20... | collective-permute-start | bytes 1769480 | tf_op jit(solution)/shard_map/ppermute | solution.py:294
  204.3 20.9 %collective-permute-start.31 = (bf16[256,768]{1,0:T(8,128)(2,1)}, bf16[256,768]{1,0:T(8,128)(2,1)}, u32[]{:S(2)}, u32[]{:S(2)}) collective-permute-start(bf16[256,768]{1,0:T(8,128)(2,1)} %subtract_convert_fusion), channel_id=1, source_target_pairs={{0,2},{1,3},{2,0},{3,1},{4,6},{5,7},{6,4},{7,5},{8,10},{9,11},{10,... | collective-permute-start | bytes 1179656 | tf_op jit(solution)/shard_map/ppermute | solution.py:297
  210.2 29.7 %collective-permute-start.39 = (bf16[2,192,768]{2,1,0:T(8,128)(2,1)}, bf16[2,192,768]{2,1,0:T(8,128)(2,1)}, u32[]{:S(2)}, u32[]{:S(2)}) collective-permute-start(bf16[2,192,768]{2,1,0:T(8,128)(2,1)} %fusion.28), channel_id=1, source_target_pairs={{0,8},{4,12},{8,0},{12,4},{1,9},{5,13},{9,1},{13,5},{2,10},{6,14},... | collective-permute-start | bytes 1769480 | tf_op jit(solution)/shard_map/ppermute | solution.py:285
  212.8 25.3 %collective-permute-start.33 = (bf16[2,192,768]{2,1,0:T(8,128)(2,1)}, bf16[2,192,768]{2,1,0:T(8,128)(2,1)}, u32[]{:S(2)}, u32[]{:S(2)}) collective-permute-start(bf16[2,192,768]{2,1,0:T(8,128)(2,1)} %pad_maximum_fusion.18), channel_id=1, source_target_pairs={{0,16},{16,0},{1,17},{17,1},{2,18},{18,2},{3,19},{19,3},{4,20},{20... | collective-permute-start | bytes 1769480 | tf_op jit(solution)/shard_map/ppermute | solution.py:294
  218.4 19.3 %collective-permute-start.36 = (bf16[192,1536]{1,0:T(8,128)(2,1)S(1)}, bf16[192,1536]{1,0:T(8,128)(2,1)S(1)}, u32[]{:S(2)}, u32[]{:S(2)}) collective-permute-start(bf16[192,1536]{1,0:T(8,128)(2,1)S(1)} %pad_maximum_fusion.19), channel_id=1, source_target_pairs={{0,1},{1,0},{2,3},{3,2},{4,5},{5,4},{6,7},{7,6},{8,9},{9,8},{10,11... | collective-permute-start | bytes 1769480 | tf_op jit(solution)/shard_map/ppermute | solution.py:297
  228.1 34.6 %collective-permute-start.32 = (bf16[2,256,768]{2,1,0:T(8,128)(2,1)}, bf16[2,256,768]{2,1,0:T(8,128)(2,1)}, u32[]{:S(2)}, u32[]{:S(2)}) collective-permute-start(bf16[2,256,768]{2,1,0:T(8,128)(2,1)} %pad_maximum_fusion.12), channel_id=1, source_target_pairs={{0,1},{1,0},{2,3},{3,2},{4,5},{5,4},{6,7},{7,6},{8,9},{9,8},{10,11... | collective-permute-start | bytes 2359304 | tf_op jit(solution)/shard_map/ppermute | solution.py:297
  239.8 15.8 %collective-permute-start.41 = (bf16[96,1536]{1,0:T(8,128)(2,1)S(1)}, bf16[96,1536]{1,0:T(8,128)(2,1)}, u32[]{:S(2)}, u32[]{:S(2)}) collective-permute-start(bf16[96,1536]{1,0:T(8,128)(2,1)S(1)} %fusion.24), channel_id=1, source_target_pairs={{0,2},{1,3},{2,0},{3,1},{4,6},{5,7},{6,4},{7,5},{8,10},{9,11},{10,... | collective-permute-start | bytes 884744 | tf_op jit(solution)/shard_map/ppermute | solution.py:297
  240.4 3.6 %collective-permute-start.44 = (f32[7680]{0:T(1024)S(1)}, f32[7680]{0:T(1024)S(1)}, u32[]{:S(2)}, u32[]{:S(2)}) collective-permute-start(f32[7680]{0:T(1024)S(1)} %constant_dynamic-update-slice_fusion.6), channel_id=1, source_target_pairs={{0,4},{4,0},{8,12},{12,8},{1,5},{5,1},{9,13},{13,9},{2,6},{6,2},{1... | collective-permute-start | bytes 92168 | tf_op jit(solution)/shard_map/ppermute | solution.py:282
  240.6 9.8 %collective-permute-start.38 = (bf16[192,768]{1,0:T(8,128)(2,1)S(1)}, bf16[192,768]{1,0:T(8,128)(2,1)S(1)}, u32[]{:S(2)}, u32[]{:S(2)}) collective-permute-start(bf16[192,768]{1,0:T(8,128)(2,1)S(1)} %pad_maximum_fusion.27), channel_id=1, source_target_pairs={{0,8},{4,12},{8,0},{12,4},{1,9},{5,13},{9,1},{13,5},{2,10},{6,14},... | collective-permute-start | bytes 884744 | tf_op jit(solution)/shard_map/ppermute | solution.py:285
  242.9 9.0 %collective-permute-start.40 = (bf16[192,768]{1,0:T(8,128)(2,1)S(1)}, bf16[192,768]{1,0:T(8,128)(2,1)S(1)}, u32[]{:S(2)}, u32[]{:S(2)}) collective-permute-start(bf16[192,768]{1,0:T(8,128)(2,1)S(1)} %fusion.47), channel_id=1, source_target_pairs={{0,16},{16,0},{1,17},{17,1},{2,18},{18,2},{3,19},{19,3},{4,20},{20... | collective-permute-start | bytes 884744 | tf_op jit(solution)/shard_map/ppermute | solution.py:294
  244.0 14.5 %collective-permute-start.45 = (f32[7680]{0:T(1024)S(1)}, f32[7680]{0:T(1024)S(1)}, u32[]{:S(2)}, u32[]{:S(2)}) collective-permute-start(f32[7680]{0:T(1024)S(1)} %add.312), channel_id=1, source_target_pairs={{0,8},{4,12},{8,0},{12,4},{1,9},{5,13},{9,1},{13,5},{2,10},{6,14},... | collective-permute-start | bytes 92168 | tf_op jit(solution)/shard_map/ppermute | solution.py:285
  255.6 11.8 %collective-permute-start.42 = (bf16[192,768]{1,0:T(8,128)(2,1)}, bf16[192,768]{1,0:T(8,128)(2,1)}, u32[]{:S(2)}, u32[]{:S(2)}) collective-permute-start(bf16[192,768]{1,0:T(8,128)(2,1)} %pad_maximum_fusion.28), channel_id=1, source_target_pairs={{0,1},{1,0},{2,3},{3,2},{4,5},{5,4},{6,7},{7,6},{8,9},{9,8},{10,11... | collective-permute-start | bytes 884744 | tf_op jit(solution)/shard_map/ppermute | solution.py:297
  258.6 4.0 %collective-permute-start.46 = (f32[7680]{0:T(1024)S(1)}, f32[7680]{0:T(1024)S(1)}, u32[]{:S(2)}, u32[]{:S(2)}) collective-permute-start(f32[7680]{0:T(1024)S(1)} %add.313), channel_id=1, source_target_pairs={{0,16},{16,0},{1,17},{17,1},{2,18},{18,2},{3,19},{19,3},{4,20},{20... | collective-permute-start | bytes 92168 | tf_op jit(solution)/shard_map/ppermute | solution.py:294
  262.6 6.0 %collective-permute-start.47 = (f32[7680]{0:T(1024)S(1)}, f32[7680]{0:T(1024)S(1)}, u32[]{:S(2)}, u32[]{:S(2)}) collective-permute-start(f32[7680]{0:T(1024)S(1)} %add.314), channel_id=1, source_target_pairs={{0,1},{1,0},{2,3},{3,2},{4,5},{5,4},{6,7},{7,6},{8,9},{9,8},{10,11... | collective-permute-start | bytes 92168 | tf_op jit(solution)/shard_map/ppermute | solution.py:297
  268.5 4.9 %collective-permute-start.48 = (f32[7680]{0:T(1024)S(1)}, f32[7680]{0:T(1024)S(1)}, u32[]{:S(2)}, u32[]{:S(2)}) collective-permute-start(f32[7680]{0:T(1024)S(1)} %add.315), channel_id=1, source_target_pairs={{0,2},{1,3},{2,0},{3,1},{4,6},{5,7},{6,4},{7,5},{8,10},{9,11},{10,... | collective-permute-start | bytes 92168 | tf_op jit(solution)/shard_map/ppermute | solution.py:297
  269.0 6.5 %collective-permute-start.43 = (bf16[96,768]{1,0:T(8,128)(2,1)S(1)}, bf16[96,768]{1,0:T(8,128)(2,1)S(1)}, u32[]{:S(2)}, u32[]{:S(2)}) collective-permute-start(bf16[96,768]{1,0:T(8,128)(2,1)S(1)} %fusion.52), channel_id=1, source_target_pairs={{0,4},{4,0},{8,12},{12,8},{1,5},{5,1},{9,13},{13,9},{2,6},{6,2},{1... | collective-permute-start | bytes 442376 | tf_op jit(solution)/shard_map/ppermute | solution.py:282
  276.1 8.2 %collective-permute-start.49 = (bf16[96,768]{1,0:T(8,128)(2,1)}, bf16[96,768]{1,0:T(8,128)(2,1)}, u32[]{:S(2)}, u32[]{:S(2)}) collective-permute-start(bf16[96,768]{1,0:T(8,128)(2,1)} %fusion.43), channel_id=1, source_target_pairs={{0,2},{1,3},{2,0},{3,1},{4,6},{5,7},{6,4},{7,5},{8,10},{9,11},{10,... | collective-permute-start | bytes 442376 | tf_op jit(solution)/shard_map/ppermute | solution.py:297
  (93 other events, 436.7 us)

commit v2 on v1

--- a/solution.py
+++ b/solution.py
@@ -413,7 +413,8 @@
     piece_b = jnp.concatenate([hidden_weight, return_weight.T], 1)
     biases = jnp.concatenate([entry_bias.reshape(-1), hidden_bias])
     far_a = place.tp_swap(piece_a, 2)
-    bias_mine = jnp.where(place.home, biases, place.tp_swap(biases, 2))
+    bias_far = place.tp_swap(biases, 2)
+    bias_mine = jnp.where(place.home, biases, bias_far)
     bias_two = jnp.stack([bias_mine, place.tp_swap(bias_mine, 1)])
     bias_q = bias_two[:, :head_width].reshape(-1)
     bias_v = bias_two[:, head_width:width].reshape(-1)
@@ -422,13 +423,13 @@
     other_a = place.tp_swap(mine_a, 1)
 
     wide = narrow + 1
-    sequence = after(place.tp, other_a)
+    sequence = after(place.tp, bias_far)
     length = lax.dynamic_index_in_dim(lengths, sequence, 0, False)
     meta = jnp.stack([place.half, place.core, length, place.ctx]).astype(jnp.int32)
     tokens_low = lax.dynamic_index_in_dim(tokens, sequence, 0, False)
     cot_low = lax.dynamic_index_in_dim(cotangent, after(sequence, tokens_low), 0, False)
     stream, first_unit, first_inverse, cot_full, normed_own, own_two = prepare(
-        meta, tokens_low, cot_low, first_gain.reshape(1, wide)
+        after(meta, mine_a), tokens_low, cot_low, first_gain.reshape(1, wide)
     )
     far_own = place.half_up(normed_own)
     all_two = jnp.concatenate([own_two, place.core_swap(own_two)], 0)
@@ -462,8 +463,8 @@
     last_r = place.half_swap(shard_r)
     return_t = place.ordered(place.half, shard_r, last_r, 1)
     return_t = return_t.reshape(-1, 2 * units)
-    near = (dot(first_normed, weight_all) + bias_all).astype(LOW)
-    far_kv = (dot(far_normed, weight_kv) + bias_all[width:]).astype(LOW)
+    near = (dot(after(first_normed, half_h), weight_all) + bias_all).astype(LOW)
+    far_kv = (dot(after(far_normed, half_h), weight_kv) + bias_all[width:]).astype(LOW)
     attended, logs = attend(meta, width, near, after(far_kv, half_h, shard_r))
 
     def joined(product, left, weight):
@@ -592,7 +593,7 @@
     pieces = after(pieces, tokens_pair, mlp_sent)
     vectors = place.chip_total(after(jnp.concatenate(pieces), mlp_first))
     vectors = vectors + after(place.tp_swap(vectors, 1), heads_sum)
-    vectors = vectors + place.tp_swap(vectors, 2)
+    vectors = vectors + after(place.tp_swap(vectors, 2), heads[2])
     own = lax.dynamic_index_in_dim(vectors[4 * wide :].reshape(4, -1), place.tp, 0, False)
     return (
         result,

time: 291 us -> 282 us (0.969)
  waiting for transfers between devices: 83.9 us -> 75.1 us
    ppermute x9, waiting for transfers between devices: 32.2 us -> 19.3 us  [half_swap(): return lax.ppermute(value, 'ctx', [(i, i ^ 2) for i in range(self.n_ctx)])]
    ppermute x9, waiting for transfers between devices: 8.16 us -> 17.1 us  [shard_swap(): return lax.ppermute(value, 'shard', [(0, 1), (1, 0)])]
    ppermute x16, waiting for transfers between devices: 43.4 us -> 38.6 us  [tp_swap(): return lax.ppermute(value, 'tp', [(i, i ^ mask) for i in range(self.n_tp)])]
    unnamed x190 -> x188, local copies, waits for them, and re-layouts: 19 us -> 17.1 us
  transfers between devices with their start and end apart: 50 -> 50, of which waited for: 17 -> 20; matrix products, arithmetic and copies ran while one was open for 29% -> 31% of each run, Pallas kernels for 12% -> 13%
where the time goes in v2:
time: 282 us; the launch traced here: 280 us
  waiting for transfers between devices  75.1 us (27%)
  starting transfers between devices  46.8 us (17%)
  other arithmetic  46.6 us (17%)
  local copies, waits for them, and re-layouts  42.5 us (15%)
  Pallas kernels  35.1 us (12%)
  matrix products  31.8 us (11%)
    ppermute x16, waiting for transfers between devices, tp_swap(): return lax.ppermute(value, 'tp', [(i, i ^ mask) for i in range(self.n_tp)])  38.6 us
    pallas_call x3, Pallas kernels, attention_call(): pl.pallas_call(kernel, grid_spec=pltpu.PrefetchScalarGridSpec(num_scalar_...  30.8 us
    ppermute x9, waiting for transfers between devices, half_swap(): return lax.ppermute(value, 'ctx', [(i, i ^ 2) for i in range(self.n_ctx)])  19.3 us
    ppermute x16, starting transfers between devices, tp_swap(): return lax.ppermute(value, 'tp', [(i, i ^ mask) for i in range(self.n_tp)])  18.1 us
    ppermute x9, waiting for transfers between devices, shard_swap(): return lax.ppermute(value, 'shard', [(0, 1), (1, 0)])  17.1 us
    unnamed x188, local copies, waits for them, and re-layouts  17.1 us
    dot_general x10, matrix products, dot_nt(): lax.dot_general(left, right, (((1,), (1,)), ((), ())), preferred_element_...  15 us
    another operation x28, other arithmetic, ordered(): return jnp.stack([first, second], axis)  14.6 us
  transfers between devices with their start and end apart: 50, of which 20 were waited for; matrix products, arithmetic and copies ran while one was open for 31% of the time, Pallas kernels for 13%

profile of v2, /device:TPU:0, one launch (start us, length us, event | category | flops | bytes accessed | tf_op | source)
XLA Modules:
  0.0 280.4 jit_solution(7841462577567714591)
XLA Ops:
  2.3 4.1 %collective-permute-start = (f32[1152]{0:T(1024)S(1)}, f32[1152]{0:T(1024)S(1)}, u32[]{:S(2)}, u32[]{:S(2)}) collective-permute-start(f32[1152]{0:T(1024)S(1)} %constant_dynamic-update-slice_fusion.13), channel_id=1, source_target_pairs={{0,2},{1,3},{2,0},{3,1},{4,6},{5,7},{6,4},{7,5},{8,10},{9,11},{10,... | collective-permute-start | bytes 13832 | tf_op jit(solution)/shard_map/ppermute | solution.py:297
  11.4 1.8 copy.33
  13.8 1.9 collective-permute-start.13
  15.7 2.2 constant_dynamic-slice_fusion.1
  19.4 1.8 copy.34
  23.1 4.3 %prepare.1 = (f32[256,768]{1,0:T(8,128)}, f32[256,768]{1,0:T(8,128)}, f32[256,1]{1,0:T(8,128)}, f32[256,768]{1,0:T(8,128)}, bf16[256,768]{1,0:T(8,128)(2,1)}, /*index=5*/bf16[256,1536]{1,0:T(8,128)(2,1)}) custom-call(s32[4]{0:T(128)} %pad_add_fusion.meta, bf16[256,767]{1,0:T(8,128)(2,1)} %bitcast.214, bf16[256,767]{1,0:T(8,128)(2,1)} %bitcast.215, ...), custom_call_target="tpu_custom_call" | custom-call | flops 3932160 | bytes 3932160 | tf_op jit(solution)/shard_map/prepare/pallas_call | solution.py:105
  27.4 3.8 %collective-permute-start.14 = (bf16[256,768]{1,0:T(8,128)(2,1)}, bf16[256,768]{1,0:T(8,128)(2,1)S(1)}, u32[]{:S(2)}, u32[]{:S(2)}) collective-permute-start(bf16[256,768]{1,0:T(8,128)(2,1)} %get-tuple-element.81), channel_id=1, source_target_pairs={{0,8},{4,12},{1,9},{5,13},{2,10},{6,14},{3,11},{7,15},{16,24},{20,... | collective-permute-start | bytes 1179656 | tf_op jit(solution)/shard_map/ppermute | solution.py:288
  31.7 2.6 collective-permute-start.5
  34.6 1.6 collective-permute-start.10
  36.3 1.6 collective-permute-start.8
  37.9 10.2 %collective-permute-done.5 = bf16[96,1536]{1,0:T(8,128)(2,1)S(1)} collective-permute-done((bf16[96,1536]{1,0:T(8,128)(2,1)S(1)}, bf16[96,1536]{1,0:T(8,128)(2,1)S(1)}, u32[]{:S(2)}, u32[]{:S(2)}) %collective-permute-start.5) | collective-permute-done | bytes 294944 | tf_op jit(solution)/shard_map/ppermute | solution.py:297
  49.6 1.6 collective-permute-start.9
  51.4 12.8 %collective-permute-done.11 = bf16[2,192,768]{2,1,0:T(8,128)(2,1)S(1)} collective-permute-done((bf16[2,192,768]{2,1,0:T(8,128)(2,1)S(1)}, bf16[2,192,768]{2,1,0:T(8,128)(2,1)S(1)}, u32[]{:S(2)}, u32[]{:S(2)}) %collective-permute-start.11) | collective-permute-done | bytes 589856 | tf_op jit(solution)/shard_map/ppermute | solution.py:285
  69.8 11.7 %collective-permute-done.16 = bf16[192,1536]{1,0:T(8,128)(2,1)S(1)} collective-permute-done((bf16[192,1536]{1,0:T(8,128)(2,1)S(1)}, bf16[192,1536]{1,0:T(8,128)(2,1)S(1)}, u32[]{:S(2)}, u32[]{:S(2)}) %collective-permute-start.16) | collective-permute-done | bytes 589856 | tf_op jit(solution)/shard_map/ppermute | solution.py:294
  86.7 1.7 add_convert_fusion.kf_ref.vf_ref.k_ref.v_ref
  88.4 2.2 fusion.7.q_ref.k_ref.v_ref
  90.6 13.4 %attend.1 = (bf16[512,384]{1,0:T(8,128)(2,1)}, f32[3,2,512]{2,1,0:T(2,128)}) custom-call(s32[4]{0:T(128)} %pad_add_fusion.meta, bf16[512,1152]{1,0:T(8,128)(2,1)} %fusion.7.q_ref.k_ref.v_ref, bf16[512,1152]{1,0:T(8,128)(2,1)} %fusion.7.q_ref.k_ref.v_ref, bf16[512,1152]{1,0:T(8,128)(2,1)} %fusion.7.q_ref.k_ref.v_ref, ...), custom_call_target="tpu_custom_call" | custom-call | flops 805306368 | bytes 3145728 | tf_op jit(solution)/shard_map/attend/pallas_call | solution.py:217
  104.0 2.4 convolution_convert_fusion.5
  109.5 3.3 %collective-permute-done.18 = bf16[2,192,1536]{2,1,0:T(8,128)(2,1)} collective-permute-done((bf16[2,192,1536]{2,1,0:T(8,128)(2,1)}, bf16[2,192,1536]{2,1,0:T(8,128)(2,1)}, u32[]{:S(2)}, u32[]{:S(2)}) %collective-permute-start.18) | collective-permute-done | bytes 1179680 | tf_op jit(solution)/shard_map/ppermute | solution.py:294
  112.8 1.5 fusion.32
  116.0 1.6 select_bitcast_fusion.1
  117.6 1.4 select_bitcast_fusion.3
  119.5 2.0 multiply_convert_fusion
  124.1 3.9 %convert_reduce_fusion = (f32[1536]{0:T(1024)S(1)}, bf16[512,1536]{1,0:T(8,128)(2,1)}) fusion(f32[512,1536]{1,0:T(8,128)S(1)} %get-tuple-element.244, bf16[768,1536]{1,0:T(8,128)(2,1)S(1)} %bitcast.209, bf16[512,1536]{1,0:T(8,128)(2,1)S(1)} %copy-done.23), kind=kOutput, calls=%fused_computation.11 | convolution fusion | flops 1225259520 | bytes 7870464 | tf_op jit(solution)/shard_map/dot_general | solution.py:24
  128.1 2.9 %convolution_convert_fusion.3 = bf16[256,768]{1,0:T(8,128)(2,1)S(1)} fusion(bf16[768,1536]{1,0:T(8,128)(2,1)} %bitcast.205, bf16[512,1536]{1,0:T(8,128)(2,1)} %get-tuple-element.88), kind=kOutput, calls=%fused_computation.28 | convolution fusion | flops 604176384 | bytes 3538944 | tf_op jit(solution)/shard_map/dot_general | solution.py:28
  147.9 8.1 %attend_far_back.1 = (bf16[512,768]{1,0:T(8,128)(2,1)}, f32[3,2,512]{2,1,0:T(2,128)}, f32[3,128,512]{2,1,0:T(8,128)}) custom-call(s32[4]{0:T(128)} %pad_add_fusion.meta, bf16[512,1152]{1,0:T(8,128)(2,1)} %fusion.7.q_ref.k_ref.v_ref, bf16[512,768]{1,0:T(8,128)(2,1)} %add_convert_fusion.kf_ref.vf_ref.k_ref.v_ref, ...), custom_call_target="tpu_custom_call" | custom-call | flops 805306368 | bytes 3145728 | tf_op jit(solution)/shard_map/attend_far_back/pallas_call | solution.py:217
  156.0 1.6 convolution_convert_fusion.1
  159.5 1.6 select_bitcast_fusion.19
  162.1 3.0 %collective-permute-start.25 = (bf16[2,256,768]{2,1,0:T(8,128)(2,1)}, bf16[2,256,768]{2,1,0:T(8,128)(2,1)}, u32[]{:S(2)}, u32[]{:S(2)}) collective-permute-start(bf16[2,256,768]{2,1,0:T(8,128)(2,1)} %pad_maximum_fusion.11), channel_id=1, source_target_pairs={{0,1},{1,0},{2,3},{3,2},{4,5},{5,4},{6,7},{7,6},{8,9},{9,8},{10,11... | collective-permute-start | bytes 2359304 | tf_op jit(solution)/shard_map/ppermute | solution.py:297
  168.6 9.2 %attend_near_back.1 = bf16[512,1152]{1,0:T(8,128)(2,1)} custom-call(s32[4]{0:T(128)} %pad_add_fusion.meta, bf16[512,1152]{1,0:T(8,128)(2,1)} %fusion.7.q_ref.k_ref.v_ref, bf16[512,1152]{1,0:T(8,128)(2,1)} %fusion.7.q_ref.k_ref.v_ref, bf16[512,1152]{1,0:T(8,128)(2,1)} %fusion.7.q_ref.k_ref.v_ref, bf16[512,384]{1,0:T(8,128)(2,1)} %convolution_convert_fusion.2.grad_ref, ...), custom_call_target="tpu_custom_call" | custom-call | flops 805306368 | bytes 3145728 | tf_op jit(solution)/shard_map/attend_near_back/pallas_call | solution.py:217
  177.9 1.9 convolution_convert_fusion
  179.8 1.8 fusion.30
  181.7 2.3 bitcast_add_fusion
  185.0 3.4 %collective-permute-start.35 = (bf16[192,1536]{1,0:T(8,128)(2,1)}, bf16[192,1536]{1,0:T(8,128)(2,1)}, u32[]{:S(2)}, u32[]{:S(2)}) collective-permute-start(bf16[192,1536]{1,0:T(8,128)(2,1)} %fusion.27), channel_id=1, source_target_pairs={{0,8},{4,12},{8,0},{12,4},{1,9},{5,13},{9,1},{13,5},{2,10},{6,14},... | collective-permute-start | bytes 1769480 | tf_op jit(solution)/shard_map/ppermute | solution.py:285
  188.5 1.6 bitcast_add_fusion.1
  192.0 1.9 multiply_reduce_fusion.1
  205.9 1.6 bitcast_add_fusion.3
  207.5 2.0 bitcast_add_fusion.4
  210.7 6.1 %collective-permute-done.31 = bf16[256,768]{1,0:T(8,128)(2,1)} collective-permute-done((bf16[256,768]{1,0:T(8,128)(2,1)}, bf16[256,768]{1,0:T(8,128)(2,1)}, u32[]{:S(2)}, u32[]{:S(2)}) %collective-permute-start.31) | collective-permute-done | bytes 393248 | tf_op jit(solution)/shard_map/ppermute | solution.py:297
  222.5 6.9 %collective-permute-done.36 = bf16[192,1536]{1,0:T(8,128)(2,1)S(1)} collective-permute-done((bf16[192,1536]{1,0:T(8,128)(2,1)S(1)}, bf16[192,1536]{1,0:T(8,128)(2,1)S(1)}, u32[]{:S(2)}, u32[]{:S(2)}) %collective-permute-start.36) | collective-permute-done | bytes 589856 | tf_op jit(solution)/shard_map/ppermute | solution.py:297
  229.7 1.6 fusion.67
  236.9 5.1 %collective-permute-done.38 = bf16[192,768]{1,0:T(8,128)(2,1)S(1)} collective-permute-done((bf16[192,768]{1,0:T(8,128)(2,1)S(1)}, bf16[192,768]{1,0:T(8,128)(2,1)S(1)}, u32[]{:S(2)}, u32[]{:S(2)}) %collective-permute-start.38) | collective-permute-done | bytes 294944 | tf_op jit(solution)/shard_map/ppermute | solution.py:285
  246.5 4.2 %collective-permute-start.42 = (bf16[192,768]{1,0:T(8,128)(2,1)}, bf16[192,768]{1,0:T(8,128)(2,1)}, u32[]{:S(2)}, u32[]{:S(2)}) collective-permute-start(bf16[192,768]{1,0:T(8,128)(2,1)} %pad_maximum_fusion.28), channel_id=1, source_target_pairs={{0,1},{1,0},{2,3},{3,2},{4,5},{5,4},{6,7},{7,6},{8,9},{9,8},{10,11... | collective-permute-start | bytes 884744 | tf_op jit(solution)/shard_map/ppermute | solution.py:297
  251.8 2.2 copy.40
  254.8 4.2 %collective-permute-done.42 = bf16[192,768]{1,0:T(8,128)(2,1)} collective-permute-done((bf16[192,768]{1,0:T(8,128)(2,1)}, bf16[192,768]{1,0:T(8,128)(2,1)}, u32[]{:S(2)}, u32[]{:S(2)}) %collective-permute-start.42) | collective-permute-done | bytes 294944 | tf_op jit(solution)/shard_map/ppermute | solution.py:297
  260.3 4.7 %collective-permute-done.48 = f32[7680]{0:T(1024)S(1)} collective-permute-done((f32[7680]{0:T(1024)S(1)}, f32[7680]{0:T(1024)S(1)}, u32[]{:S(2)}, u32[]{:S(2)}) %collective-permute-start.48) | collective-permute-done | bytes 30752 | tf_op jit(solution)/shard_map/ppermute | solution.py:297
  269.3 2.2 copy.41
  271.5 4.1 %collective-permute-done.49 = bf16[96,768]{1,0:T(8,128)(2,1)} collective-permute-done((bf16[96,768]{1,0:T(8,128)(2,1)}, bf16[96,768]{1,0:T(8,128)(2,1)}, u32[]{:S(2)}, u32[]{:S(2)}) %collective-permute-start.49) | collective-permute-done | bytes 147488 | tf_op jit(solution)/shard_map/ppermute | solution.py:297
  (427 shorter events, 98.4 us)
Async XLA Ops:
  2.3 8.3 %collective-permute-start = (f32[1152]{0:T(1024)S(1)}, f32[1152]{0:T(1024)S(1)}, u32[]{:S(2)}, u32[]{:S(2)}) collective-permute-start(f32[1152]{0:T(1024)S(1)} %constant_dynamic-update-slice_fusion.13), channel_id=1, source_target_pairs={{0,2},{1,3},{2,0},{3,1},{4,6},{5,7},{6,4},{7,5},{8,10},{9,11},{10,... | collective-permute-start | bytes 13832 | tf_op jit(solution)/shard_map/ppermute | solution.py:297
  8.2 9.8 %collective-permute-start.1 = (bf16[96,768]{1,0:T(8,128)(2,1)S(1)}, bf16[96,768]{1,0:T(8,128)(2,1)S(1)}, u32[]{:S(2)}, u32[]{:S(2)}) collective-permute-start(bf16[96,768]{1,0:T(8,128)(2,1)S(1)} %pad_maximum_fusion.30), channel_id=1, source_target_pairs={{0,2},{1,3},{2,0},{3,1},{4,6},{5,7},{6,4},{7,5},{8,10},{9,11},{10,... | collective-permute-start | bytes 442376 | tf_op jit(solution)/shard_map/ppermute | solution.py:297
  13.8 7.4 %collective-permute-start.13 = (f32[1152]{0:T(1024)S(1)}, f32[1152]{0:T(1024)S(1)}, u32[]{:S(2)}, u32[]{:S(2)}) collective-permute-start(f32[1152]{0:T(1024)S(1)} %broadcast_select_fusion.12), channel_id=1, source_target_pairs={{0,1},{1,0},{2,3},{3,2},{4,5},{5,4},{6,7},{7,6},{8,9},{9,8},{10,11... | collective-permute-start | bytes 13832 | tf_op jit(solution)/shard_map/ppermute | solution.py:297
  18.1 4.0 %collective-permute-start.2 = (bf16[96,768]{1,0:T(8,128)(2,1)S(1)}, bf16[96,768]{1,0:T(8,128)(2,1)S(1)}, u32[]{:S(2)}, u32[]{:S(2)}) collective-permute-start(bf16[96,768]{1,0:T(8,128)(2,1)S(1)} %broadcast_select_fusion.2), channel_id=1, source_target_pairs={{0,4},{4,0},{8,12},{12,8},{1,5},{5,1},{9,13},{13,9},{2,6},{6,2},{1... | collective-permute-start | bytes 442376 | tf_op jit(solution)/shard_map/ppermute | solution.py:282
  22.3 9.5 %collective-permute-start.4 = (bf16[192,768]{1,0:T(8,128)(2,1)S(1)}, bf16[192,768]{1,0:T(8,128)(2,1)S(1)}, u32[]{:S(2)}, u32[]{:S(2)}) collective-permute-start(bf16[192,768]{1,0:T(8,128)(2,1)S(1)} %bitcast.212), channel_id=1, source_target_pairs={{0,1},{1,0},{2,3},{3,2},{4,5},{5,4},{6,7},{7,6},{8,9},{9,8},{10,11... | collective-permute-start | bytes 884744 | tf_op jit(solution)/shard_map/ppermute | solution.py:297
  27.4 38.1 %collective-permute-start.14 = (bf16[256,768]{1,0:T(8,128)(2,1)}, bf16[256,768]{1,0:T(8,128)(2,1)S(1)}, u32[]{:S(2)}, u32[]{:S(2)}) collective-permute-start(bf16[256,768]{1,0:T(8,128)(2,1)} %get-tuple-element.81), channel_id=1, source_target_pairs={{0,8},{4,12},{1,9},{5,13},{2,10},{6,14},{3,11},{7,15},{16,24},{20,... | collective-permute-start | bytes 1179656 | tf_op jit(solution)/shard_map/ppermute | solution.py:288
  31.1 36.2 %collective-permute-start.3 = (bf16[256,1536]{1,0:T(8,128)(2,1)}, bf16[256,1536]{1,0:T(8,128)(2,1)S(1)}, u32[]{:S(2)}, u32[]{:S(2)}) collective-permute-start(bf16[256,1536]{1,0:T(8,128)(2,1)} %get-tuple-element.77), channel_id=1, source_target_pairs={{0,4},{4,0},{8,12},{12,8},{1,5},{5,1},{9,13},{13,9},{2,6},{6,2},{1... | collective-permute-start | bytes 2359304 | tf_op jit(solution)/shard_map/ppermute | solution.py:282
  31.7 16.3 %collective-permute-start.5 = (bf16[96,1536]{1,0:T(8,128)(2,1)S(1)}, bf16[96,1536]{1,0:T(8,128)(2,1)S(1)}, u32[]{:S(2)}, u32[]{:S(2)}) collective-permute-start(bf16[96,1536]{1,0:T(8,128)(2,1)S(1)} %pad_maximum_fusion.24), channel_id=1, source_target_pairs={{0,2},{1,3},{2,0},{3,1},{4,6},{5,7},{6,4},{7,5},{8,10},{9,11},{10,... | collective-permute-start | bytes 884744 | tf_op jit(solution)/shard_map/ppermute | solution.py:297
  34.6 13.6 %collective-permute-start.10 = (bf16[192,768]{1,0:T(8,128)(2,1)S(1)}, bf16[192,768]{1,0:T(8,128)(2,1)S(1)}, u32[]{:S(2)}, u32[]{:S(2)}) collective-permute-start(bf16[192,768]{1,0:T(8,128)(2,1)S(1)} %pad_maximum_fusion.26), channel_id=1, source_target_pairs={{0,16},{16,0},{1,17},{17,1},{2,18},{18,2},{3,19},{19,3},{4,20},{20... | collective-permute-start | bytes 884744 | tf_op jit(solution)/shard_map/ppermute | solution.py:294
  36.3 13.1 %collective-permute-start.8 = (bf16[192,768]{1,0:T(8,128)(2,1)S(1)}, bf16[192,768]{1,0:T(8,128)(2,1)S(1)}, u32[]{:S(2)}, u32[]{:S(2)}) collective-permute-start(bf16[192,768]{1,0:T(8,128)(2,1)S(1)} %pad_maximum_fusion.25), channel_id=1, source_target_pairs={{0,8},{4,12},{8,0},{12,4},{1,9},{5,13},{9,1},{13,5},{2,10},{6,14},... | collective-permute-start | bytes 884744 | tf_op jit(solution)/shard_map/ppermute | solution.py:285
  48.1 3.1 %collective-permute-start.6 = (bf16[96,1536]{1,0:T(8,128)(2,1)S(1)}, bf16[96,1536]{1,0:T(8,128)(2,1)S(1)}, u32[]{:S(2)}, u32[]{:S(2)}) collective-permute-start(bf16[96,1536]{1,0:T(8,128)(2,1)S(1)} %broadcast_select_fusion), channel_id=1, source_target_pairs={{0,4},{4,0},{8,12},{12,8},{1,5},{5,1},{9,13},{13,9},{2,6},{6,2},{1... | collective-permute-start | bytes 884744 | tf_op jit(solution)/shard_map/ppermute | solution.py:282
  48.4 15.8 %collective-permute-start.11 = (bf16[2,192,768]{2,1,0:T(8,128)(2,1)S(1)}, bf16[2,192,768]{2,1,0:T(8,128)(2,1)S(1)}, u32[]{:S(2)}, u32[]{:S(2)}) collective-permute-start(bf16[2,192,768]{2,1,0:T(8,128)(2,1)S(1)} %pad_maximum_fusion.17), channel_id=1, source_target_pairs={{0,8},{4,12},{8,0},{12,4},{1,9},{5,13},{9,1},{13,5},{2,10},{6,14},... | collective-permute-start | bytes 1769480 | tf_op jit(solution)/shard_map/ppermute | solution.py:285
  49.6 15.5 %collective-permute-start.9 = (bf16[2,192,768]{2,1,0:T(8,128)(2,1)S(1)}, bf16[2,192,768]{2,1,0:T(8,128)(2,1)S(1)}, u32[]{:S(2)}, u32[]{:S(2)}) collective-permute-start(bf16[2,192,768]{2,1,0:T(8,128)(2,1)S(1)} %pad_maximum_fusion.16), channel_id=1, source_target_pairs={{0,16},{16,0},{1,17},{17,1},{2,18},{18,2},{3,19},{19,3},{4,20},{20... | collective-permute-start | bytes 1769480 | tf_op jit(solution)/shard_map/ppermute | solution.py:294
  51.3 15.2 %collective-permute-start.7 = (bf16[192,1536]{1,0:T(8,128)(2,1)S(1)}, bf16[192,1536]{1,0:T(8,128)(2,1)S(1)}, u32[]{:S(2)}, u32[]{:S(2)}) collective-permute-start(bf16[192,1536]{1,0:T(8,128)(2,1)S(1)} %bitcast.210), channel_id=1, source_target_pairs={{0,1},{1,0},{2,3},{3,2},{4,5},{5,4},{6,7},{7,6},{8,9},{9,8},{10,11... | collective-permute-start | bytes 1769480 | tf_op jit(solution)/shard_map/ppermute | solution.py:297
  65.5 4.3 %collective-permute-start.15 = (bf16[256,768]{1,0:T(8,128)(2,1)S(1)}, bf16[256,768]{1,0:T(8,128)(2,1)S(1)}, u32[]{:S(2)}, u32[]{:S(2)}) collective-permute-start(bf16[256,768]{1,0:T(8,128)(2,1)S(1)} %collective-permute-done.14), channel_id=1, source_target_pairs={{0,4},{4,0},{8,12},{12,8},{1,5},{5,1},{9,13},{13,9},{2,6},{6,2},{1... | collective-permute-start | bytes 1179656 | tf_op jit(solution)/shard_map/ppermute | solution.py:282
  66.7 14.8 %collective-permute-start.16 = (bf16[192,1536]{1,0:T(8,128)(2,1)S(1)}, bf16[192,1536]{1,0:T(8,128)(2,1)S(1)}, u32[]{:S(2)}, u32[]{:S(2)}) collective-permute-start(bf16[192,1536]{1,0:T(8,128)(2,1)S(1)} %get-tuple-element.84), channel_id=1, source_target_pairs={{0,16},{16,0},{1,17},{17,1},{2,18},{18,2},{3,19},{19,3},{4,20},{20... | collective-permute-start | bytes 1769480 | tf_op jit(solution)/shard_map/ppermute | solution.py:294
  68.6 15.4 %collective-permute-start.12 = (bf16[192,1536]{1,0:T(8,128)(2,1)S(1)}, bf16[192,1536]{1,0:T(8,128)(2,1)S(1)}, u32[]{:S(2)}, u32[]{:S(2)}) collective-permute-start(bf16[192,1536]{1,0:T(8,128)(2,1)S(1)} %get-tuple-element.79), channel_id=1, source_target_pairs={{0,8},{4,12},{8,0},{12,4},{1,9},{5,13},{9,1},{13,5},{2,10},{6,14},... | collective-permute-start | bytes 1769480 | tf_op jit(solution)/shard_map/ppermute | solution.py:285
  82.7 26.8 %collective-permute-start.19 = (bf16[2,192,1536]{2,1,0:T(8,128)(2,1)}, bf16[2,192,1536]{2,1,0:T(8,128)(2,1)}, u32[]{:S(2)}, u32[]{:S(2)}) collective-permute-start(bf16[2,192,1536]{2,1,0:T(8,128)(2,1)} %pad_maximum_fusion.8), channel_id=1, source_target_pairs={{0,8},{4,12},{8,0},{12,4},{1,9},{5,13},{9,1},{13,5},{2,10},{6,14},... | collective-permute-start | bytes 3538952 | tf_op jit(solution)/shard_map/ppermute | solution.py:285
  85.3 27.5 %collective-permute-start.18 = (bf16[2,192,1536]{2,1,0:T(8,128)(2,1)}, bf16[2,192,1536]{2,1,0:T(8,128)(2,1)}, u32[]{:S(2)}, u32[]{:S(2)}) collective-permute-start(bf16[2,192,1536]{2,1,0:T(8,128)(2,1)} %pad_maximum_fusion.7), channel_id=1, source_target_pairs={{0,16},{16,0},{1,17},{17,1},{2,18},{18,2},{3,19},{19,3},{4,20},{20... | collective-permute-start | bytes 3538952 | tf_op jit(solution)/shard_map/ppermute | solution.py:294
  115.9 3.6 %collective-permute-start.20 = (bf16[256,768]{1,0:T(8,128)(2,1)S(1)}, bf16[256,768]{1,0:T(8,128)(2,1)S(1)}, u32[]{:S(2)}, u32[]{:S(2)}) collective-permute-start(bf16[256,768]{1,0:T(8,128)(2,1)S(1)} %multiply_convert_fusion.1), channel_id=1, source_target_pairs={{0,4},{4,0},{8,12},{12,8},{1,5},{5,1},{9,13},{13,9},{2,6},{6,2},{1... | collective-permute-start | bytes 1179656 | tf_op jit(solution)/shard_map/ppermute | solution.py:282
  130.9 3.5 %collective-permute-start.23 = (bf16[256,768]{1,0:T(8,128)(2,1)S(1)}, bf16[256,768]{1,0:T(8,128)(2,1)S(1)}, u32[]{:S(2)}, u32[]{:S(2)}) collective-permute-start(bf16[256,768]{1,0:T(8,128)(2,1)S(1)} %convolution_convert_fusion.3), channel_id=1, source_target_pairs={{0,4},{4,0},{8,12},{12,8},{1,5},{5,1},{9,13},{13,9},{2,6},{6,2},{1... | collective-permute-start | bytes 1179656 | tf_op jit(solution)/shard_map/ppermute | solution.py:282
  131.3 2.0 collective-permute-start.21
  136.2 10.3 %collective-permute-start.24 = (bf16[256,768]{1,0:T(8,128)(2,1)S(1)}, bf16[256,768]{1,0:T(8,128)(2,1)S(1)}, u32[]{:S(2)}, u32[]{:S(2)}) collective-permute-start(bf16[256,768]{1,0:T(8,128)(2,1)S(1)} %get-tuple-element.171), channel_id=1, source_target_pairs={{0,4},{4,0},{8,12},{12,8},{1,5},{5,1},{9,13},{13,9},{2,6},{6,2},{1... | collective-permute-start | bytes 1179656 | tf_op jit(solution)/shard_map/ppermute | solution.py:282
  136.5 23.0 %collective-permute-start.22 = (bf16[256,768]{1,0:T(8,128)(2,1)}, bf16[256,768]{1,0:T(8,128)(2,1)}, u32[]{:S(2)}, u32[]{:S(2)}) collective-permute-start(bf16[256,768]{1,0:T(8,128)(2,1)} %subtract_convert_fusion.2), channel_id=1, source_target_pairs={{0,2},{1,3},{2,0},{3,1},{4,6},{5,7},{6,4},{7,5},{8,10},{9,11},{10,... | collective-permute-start | bytes 1179656 | tf_op jit(solution)/shard_map/ppermute | solution.py:297
  141.6 40.0 %collective-permute-start.30 = (bf16[2,192,1536]{2,1,0:T(8,128)(2,1)}, bf16[2,192,1536]{2,1,0:T(8,128)(2,1)}, u32[]{:S(2)}, u32[]{:S(2)}) collective-permute-start(bf16[2,192,1536]{2,1,0:T(8,128)(2,1)} %fusion.9), channel_id=1, source_target_pairs={{0,16},{16,0},{1,17},{17,1},{2,18},{18,2},{3,19},{19,3},{4,20},{20... | collective-permute-start | bytes 3538952 | tf_op jit(solution)/shard_map/ppermute | solution.py:294
  145.6 42.8 %collective-permute-start.29 = (bf16[2,192,1536]{2,1,0:T(8,128)(2,1)}, bf16[2,192,1536]{2,1,0:T(8,128)(2,1)}, u32[]{:S(2)}, u32[]{:S(2)}) collective-permute-start(bf16[2,192,1536]{2,1,0:T(8,128)(2,1)} %fusion.8), channel_id=1, source_target_pairs={{0,8},{4,12},{8,0},{12,4},{1,9},{5,13},{9,1},{13,5},{2,10},{6,14},... | collective-permute-start | bytes 3538952 | tf_op jit(solution)/shard_map/ppermute | solution.py:285
  158.2 8.4 %collective-permute-start.26 = (bf16[256,768]{1,0:T(8,128)(2,1)S(1)}, bf16[256,768]{1,0:T(8,128)(2,1)S(1)}, u32[]{:S(2)}, u32[]{:S(2)}) collective-permute-start(bf16[256,768]{1,0:T(8,128)(2,1)S(1)} %convolution_convert_fusion.1), channel_id=1, source_target_pairs={{0,4},{4,0},{8,12},{12,8},{1,5},{5,1},{9,13},{13,9},{2,6},{6,2},{1... | collective-permute-start | bytes 1179656 | tf_op jit(solution)/shard_map/ppermute | solution.py:282
  162.1 26.2 %collective-permute-start.25 = (bf16[2,256,768]{2,1,0:T(8,128)(2,1)}, bf16[2,256,768]{2,1,0:T(8,128)(2,1)}, u32[]{:S(2)}, u32[]{:S(2)}) collective-permute-start(bf16[2,256,768]{2,1,0:T(8,128)(2,1)} %pad_maximum_fusion.11), channel_id=1, source_target_pairs={{0,1},{1,0},{2,3},{3,2},{4,5},{5,4},{6,7},{7,6},{8,9},{9,8},{10,11... | collective-permute-start | bytes 2359304 | tf_op jit(solution)/shard_map/ppermute | solution.py:297
  167.3 21.0 %collective-permute-start.27 = (bf16[256,768]{1,0:T(8,128)(2,1)}, bf16[256,768]{1,0:T(8,128)(2,1)}, u32[]{:S(2)}, u32[]{:S(2)}) collective-permute-start(bf16[256,768]{1,0:T(8,128)(2,1)} %add_convert_fusion.1), channel_id=1, source_target_pairs={{8,0},{12,4},{9,1},{13,5},{10,2},{14,6},{11,3},{15,7},{24,16},{28,... | collective-permute-start | bytes 1179656 | tf_op jit(solution)/shard_map/ppermute | solution.py:291
  185.0 20.9 %collective-permute-start.35 = (bf16[192,1536]{1,0:T(8,128)(2,1)}, bf16[192,1536]{1,0:T(8,128)(2,1)}, u32[]{:S(2)}, u32[]{:S(2)}) collective-permute-start(bf16[192,1536]{1,0:T(8,128)(2,1)} %fusion.27), channel_id=1, source_target_pairs={{0,8},{4,12},{8,0},{12,4},{1,9},{5,13},{9,1},{13,5},{2,10},{6,14},... | collective-permute-start | bytes 1769480 | tf_op jit(solution)/shard_map/ppermute | solution.py:285
  188.4 3.6 %collective-permute-start.28 = (bf16[256,768]{1,0:T(8,128)(2,1)S(1)}, bf16[256,768]{1,0:T(8,128)(2,1)S(1)}, u32[]{:S(2)}, u32[]{:S(2)}) collective-permute-start(bf16[256,768]{1,0:T(8,128)(2,1)S(1)} %convolution_convert_fusion), channel_id=1, source_target_pairs={{0,4},{4,0},{8,12},{12,8},{1,5},{5,1},{9,13},{13,9},{2,6},{6,2},{1... | collective-permute-start | bytes 1179656 | tf_op jit(solution)/shard_map/ppermute | solution.py:282
  191.1 16.4 %collective-permute-start.34 = (bf16[192,1536]{1,0:T(8,128)(2,1)}, bf16[192,1536]{1,0:T(8,128)(2,1)}, u32[]{:S(2)}, u32[]{:S(2)}) collective-permute-start(bf16[192,1536]{1,0:T(8,128)(2,1)} %fusion.26), channel_id=1, source_target_pairs={{0,16},{16,0},{1,17},{17,1},{2,18},{18,2},{3,19},{19,3},{4,20},{20... | collective-permute-start | bytes 1769480 | tf_op jit(solution)/shard_map/ppermute | solution.py:294
  196.3 20.5 %collective-permute-start.31 = (bf16[256,768]{1,0:T(8,128)(2,1)}, bf16[256,768]{1,0:T(8,128)(2,1)}, u32[]{:S(2)}, u32[]{:S(2)}) collective-permute-start(bf16[256,768]{1,0:T(8,128)(2,1)} %subtract_convert_fusion), channel_id=1, source_target_pairs={{0,2},{1,3},{2,0},{3,1},{4,6},{5,7},{6,4},{7,5},{8,10},{9,11},{10,... | collective-permute-start | bytes 1179656 | tf_op jit(solution)/shard_map/ppermute | solution.py:297
  202.1 29.4 %collective-permute-start.39 = (bf16[2,192,768]{2,1,0:T(8,128)(2,1)}, bf16[2,192,768]{2,1,0:T(8,128)(2,1)}, u32[]{:S(2)}, u32[]{:S(2)}) collective-permute-start(bf16[2,192,768]{2,1,0:T(8,128)(2,1)} %fusion.28), channel_id=1, source_target_pairs={{0,8},{4,12},{8,0},{12,4},{1,9},{5,13},{9,1},{13,5},{2,10},{6,14},... | collective-permute-start | bytes 1769480 | tf_op jit(solution)/shard_map/ppermute | solution.py:285
  204.6 25.1 %collective-permute-start.33 = (bf16[2,192,768]{2,1,0:T(8,128)(2,1)}, bf16[2,192,768]{2,1,0:T(8,128)(2,1)}, u32[]{:S(2)}, u32[]{:S(2)}) collective-permute-start(bf16[2,192,768]{2,1,0:T(8,128)(2,1)} %pad_maximum_fusion.18), channel_id=1, source_target_pairs={{0,16},{16,0},{1,17},{17,1},{2,18},{18,2},{3,19},{19,3},{4,20},{20... | collective-permute-start | bytes 1769480 | tf_op jit(solution)/shard_map/ppermute | solution.py:294
  210.6 18.7 %collective-permute-start.36 = (bf16[192,1536]{1,0:T(8,128)(2,1)S(1)}, bf16[192,1536]{1,0:T(8,128)(2,1)S(1)}, u32[]{:S(2)}, u32[]{:S(2)}) collective-permute-start(bf16[192,1536]{1,0:T(8,128)(2,1)S(1)} %pad_maximum_fusion.19), channel_id=1, source_target_pairs={{0,1},{1,0},{2,3},{3,2},{4,5},{5,4},{6,7},{7,6},{8,9},{9,8},{10,11... | collective-permute-start | bytes 1769480 | tf_op jit(solution)/shard_map/ppermute | solution.py:297
  219.7 35.1 %collective-permute-start.32 = (bf16[2,256,768]{2,1,0:T(8,128)(2,1)}, bf16[2,256,768]{2,1,0:T(8,128)(2,1)}, u32[]{:S(2)}, u32[]{:S(2)}) collective-permute-start(bf16[2,256,768]{2,1,0:T(8,128)(2,1)} %pad_maximum_fusion.12), channel_id=1, source_target_pairs={{0,1},{1,0},{2,3},{3,2},{4,5},{5,4},{6,7},{7,6},{8,9},{9,8},{10,11... | collective-permute-start | bytes 2359304 | tf_op jit(solution)/shard_map/ppermute | solution.py:297
  231.4 15.1 %collective-permute-start.41 = (bf16[96,1536]{1,0:T(8,128)(2,1)S(1)}, bf16[96,1536]{1,0:T(8,128)(2,1)}, u32[]{:S(2)}, u32[]{:S(2)}) collective-permute-start(bf16[96,1536]{1,0:T(8,128)(2,1)S(1)} %fusion.24), channel_id=1, source_target_pairs={{0,2},{1,3},{2,0},{3,1},{4,6},{5,7},{6,4},{7,5},{8,10},{9,11},{10,... | collective-permute-start | bytes 884744 | tf_op jit(solution)/shard_map/ppermute | solution.py:297
  232.0 3.5 %collective-permute-start.44 = (f32[7680]{0:T(1024)S(1)}, f32[7680]{0:T(1024)S(1)}, u32[]{:S(2)}, u32[]{:S(2)}) collective-permute-start(f32[7680]{0:T(1024)S(1)} %constant_dynamic-update-slice_fusion.6), channel_id=1, source_target_pairs={{0,4},{4,0},{8,12},{12,8},{1,5},{5,1},{9,13},{13,9},{2,6},{6,2},{1... | collective-permute-start | bytes 92168 | tf_op jit(solution)/shard_map/ppermute | solution.py:282
  232.2 9.8 %collective-permute-start.38 = (bf16[192,768]{1,0:T(8,128)(2,1)S(1)}, bf16[192,768]{1,0:T(8,128)(2,1)S(1)}, u32[]{:S(2)}, u32[]{:S(2)}) collective-permute-start(bf16[192,768]{1,0:T(8,128)(2,1)S(1)} %pad_maximum_fusion.27), channel_id=1, source_target_pairs={{0,8},{4,12},{8,0},{12,4},{1,9},{5,13},{9,1},{13,5},{2,10},{6,14},... | collective-permute-start | bytes 884744 | tf_op jit(solution)/shard_map/ppermute | solution.py:285
  234.5 9.2 %collective-permute-start.40 = (bf16[192,768]{1,0:T(8,128)(2,1)S(1)}, bf16[192,768]{1,0:T(8,128)(2,1)S(1)}, u32[]{:S(2)}, u32[]{:S(2)}) collective-permute-start(bf16[192,768]{1,0:T(8,128)(2,1)S(1)} %fusion.47), channel_id=1, source_target_pairs={{0,16},{16,0},{1,17},{17,1},{2,18},{18,2},{3,19},{19,3},{4,20},{20... | collective-permute-start | bytes 884744 | tf_op jit(solution)/shard_map/ppermute | solution.py:294
  235.6 15.1 %collective-permute-start.45 = (f32[7680]{0:T(1024)S(1)}, f32[7680]{0:T(1024)S(1)}, u32[]{:S(2)}, u32[]{:S(2)}) collective-permute-start(f32[7680]{0:T(1024)S(1)} %add.312), channel_id=1, source_target_pairs={{0,8},{4,12},{8,0},{12,4},{1,9},{5,13},{9,1},{13,5},{2,10},{6,14},... | collective-permute-start | bytes 92168 | tf_op jit(solution)/shard_map/ppermute | solution.py:285
  246.5 12.4 %collective-permute-start.42 = (bf16[192,768]{1,0:T(8,128)(2,1)}, bf16[192,768]{1,0:T(8,128)(2,1)}, u32[]{:S(2)}, u32[]{:S(2)}) collective-permute-start(bf16[192,768]{1,0:T(8,128)(2,1)} %pad_maximum_fusion.28), channel_id=1, source_target_pairs={{0,1},{1,0},{2,3},{3,2},{4,5},{5,4},{6,7},{7,6},{8,9},{9,8},{10,11... | collective-permute-start | bytes 884744 | tf_op jit(solution)/shard_map/ppermute | solution.py:297
  250.7 4.0 %collective-permute-start.46 = (f32[7680]{0:T(1024)S(1)}, f32[7680]{0:T(1024)S(1)}, u32[]{:S(2)}, u32[]{:S(2)}) collective-permute-start(f32[7680]{0:T(1024)S(1)} %add.313), channel_id=1, source_target_pairs={{0,16},{16,0},{1,17},{17,1},{2,18},{18,2},{3,19},{19,3},{4,20},{20... | collective-permute-start | bytes 92168 | tf_op jit(solution)/shard_map/ppermute | solution.py:294
  254.7 5.5 %collective-permute-start.47 = (f32[7680]{0:T(1024)S(1)}, f32[7680]{0:T(1024)S(1)}, u32[]{:S(2)}, u32[]{:S(2)}) collective-permute-start(f32[7680]{0:T(1024)S(1)} %add.314), channel_id=1, source_target_pairs={{0,1},{1,0},{2,3},{3,2},{4,5},{5,4},{6,7},{7,6},{8,9},{9,8},{10,11... | collective-permute-start | bytes 92168 | tf_op jit(solution)/shard_map/ppermute | solution.py:297
  260.2 4.9 %collective-permute-start.48 = (f32[7680]{0:T(1024)S(1)}, f32[7680]{0:T(1024)S(1)}, u32[]{:S(2)}, u32[]{:S(2)}) collective-permute-start(f32[7680]{0:T(1024)S(1)} %add.315), channel_id=1, source_target_pairs={{0,2},{1,3},{2,0},{3,1},{4,6},{5,7},{6,4},{7,5},{8,10},{9,11},{10,... | collective-permute-start | bytes 92168 | tf_op jit(solution)/shard_map/ppermute | solution.py:297
  260.3 6.8 %collective-permute-start.43 = (bf16[96,768]{1,0:T(8,128)(2,1)S(1)}, bf16[96,768]{1,0:T(8,128)(2,1)S(1)}, u32[]{:S(2)}, u32[]{:S(2)}) collective-permute-start(bf16[96,768]{1,0:T(8,128)(2,1)S(1)} %fusion.52), channel_id=1, source_target_pairs={{0,4},{4,0},{8,12},{12,8},{1,5},{5,1},{9,13},{13,9},{2,6},{6,2},{1... | collective-permute-start | bytes 442376 | tf_op jit(solution)/shard_map/ppermute | solution.py:282
  267.8 7.9 %collective-permute-start.49 = (bf16[96,768]{1,0:T(8,128)(2,1)}, bf16[96,768]{1,0:T(8,128)(2,1)}, u32[]{:S(2)}, u32[]{:S(2)}) collective-permute-start(bf16[96,768]{1,0:T(8,128)(2,1)} %fusion.43), channel_id=1, source_target_pairs={{0,2},{1,3},{2,0},{3,1},{4,6},{5,7},{6,4},{7,5},{8,10},{9,11},{10,... | collective-permute-start | bytes 442376 | tf_op jit(solution)/shard_map/ppermute | solution.py:297
  (92 other events, 417.6 us)
